TPU v7x, 32 devices: a whole 2x2x4 slice. The times are simulated.
32 devices in a mesh: cond: 4 (over y, x), space: 8 (over z, core).
Axes of the slice: x: 2, y: 2, z: 4, core: 2. Of those that a mesh axis runs over, the one named last changes fastest.
Arguments:
- flow: float32 [8, 3, 128, 2048], P('cond', None, 'space'), may hold values from -4 to 4
- forcing: float32 [8, 2, 128, 2048], P('cond', None, 'space'), may hold values from -4 to 4
- wet: int32 [8, 128, 2048], P('cond', 'space'), may hold values 0 or 1
- depth: float32 [128, 2048], P('space'), may hold values from 0.5 to 2
- limiter: int32 [128, 2048], P('space'), may hold values 0 or 1
- weights: int32 [8], replicated, may hold values from 1 to 9
- bed: float32 [128, 2048], P('space'), may hold values from -6 to 6
- diffusivity: float32 [128, 2048], P('space'), may hold values from 0.2 to 5
Outputs:
- surface: float32 [8, 128, 2048], P('cond', 'space')
- bed_new: float32 [128, 2048], P('space')
All inputs are finite; a program needn't handle non-finite values. No bound on the sum of `wet` or of `limiter` on one device may be relied on, other than what follows from the above.
Results may differ from a plain program's by a relative error of at most 0.0001.
Values sent between devices are 32-bit elements; how exact they have to be, the bound alone decides.
No kernel may reach another device: no remote copies, remote signals or barrier semaphores. Data moves between devices by JAX's collectives and lax.ppermute only.
A program may use at most 64 MiB of HBM per device.

v0:
```python
import jax
import jax.numpy as jnp
from jax import lax
from jax.sharding import PartitionSpec as P

STEPS = 4
ITERS = 2


time_step = 0.4
gravity = 1.0
friction = 0.1
transport_base = 0.5
morph_factor = 1.0
slope_coeff = 1.0


def with_halo(cells, sides, width):
    for axis, dim in sides:
        count = lax.axis_size(axis)
        ends = count - 1
        head = lax.slice_in_dim(cells, 0, width, axis=dim)
        tail = lax.slice_in_dim(cells, cells.shape[dim] - width, cells.shape[dim], axis=dim)
        cells = jnp.concatenate(
            [
                lax.ppermute(tail, axis, [(i, (i + 1) % count) for i in range(ends)]),
                cells,
                lax.ppermute(head, axis, [((i + 1) % count, i) for i in range(ends)]),
            ],
            axis=dim,
        )
    return cells


def rows_diff(padded):
    return 0.5 * (padded[..., 2:, :] - padded[..., :-2, :])


def column_diff(field):
    padded = jnp.pad(field, [(0, 0)] * (field.ndim - 1) + [(1, 1)])
    return 0.5 * (padded[..., 2:] - padded[..., :-2])


def paired_fields(state_now, depth):
    return [state_now[:, 0], depth * state_now[:, 1]]


def flow_rim(state_now, depth):
    paired = jnp.stack(paired_fields(state_now, depth), 1)
    return with_halo(paired, (("space", 2),), 1)


def tendency(state_now, rim_rows, depth, wet_mask, force):
    elevation, vel_first, vel_second = (state_now[:, 0], state_now[:, 1], state_now[:, 2])
    rate_elev = -(rows_diff(rim_rows[:, 1]) + column_diff(depth * vel_second))
    rate_first = -gravity * rows_diff(rim_rows[:, 0]) - friction * vel_first + force[:, 0]
    rate_second = -gravity * column_diff(elevation) - friction * vel_second + force[:, 1]
    return wet_mask * jnp.stack([rate_elev, rate_first, rate_second], 1)


def transport(state_now, limit_mask):
    vel_first, vel_second = (state_now[:, 1], state_now[:, 2])
    energy = vel_first * vel_first + vel_second * vel_second
    factor = (transport_base + energy) / (1.0 + limit_mask * energy)
    return (vel_first * factor, vel_second * factor)


def second_section(state_now, rim_rows, depth, wet_mask, forcing):
    first_section = state_now + time_step * tendency(state_now, rim_rows, depth, wet_mask, forcing)
    rim_next = flow_rim(first_section, depth)
    return 0.5 * (
        state_now
        + first_section
        + time_step * tendency(first_section, rim_next, depth, wet_mask, forcing)
    )


def rim_cells(field):
    padded = with_halo(field, (("space", 0),), 1)
    return jnp.pad(padded, ((0, 0), (1, 1)))


def reduce_all(values):
    return lax.psum(values, "space")


def neighbours(padded):
    return [padded[:-2, 1:-1], padded[2:, 1:-1], padded[1:-1, :-2], padded[1:-1, 2:]]


def apply_op(field, coefs):
    near = neighbours(rim_cells(field))
    total = coefs[0] * (field - near[0]) + coefs[1] * (field - near[1])
    total = total + coefs[2] * (field - near[2]) + coefs[3] * (field - near[3])
    return field + slope_coeff * total


def local(flow, forcing, wet, depth, limiter, weights, bed, diffusivity):
    cond_here = flow.shape[0]
    wet_mask = wet.astype(jnp.float32)[:, None]
    limit_mask = limiter.astype(jnp.float32)
    state_now = flow
    bed_change = jnp.zeros((cond_here,) + flow.shape[2:], jnp.float32)
    for stepper in range(STEPS):
        rim_rows = flow_rim(state_now, depth)
        state_now = second_section(state_now, rim_rows, depth, wet_mask, forcing)
        flux_first, flux_second = transport(state_now, limit_mask)
        flux_rows = with_halo(flux_first, (("space", 1),), 1)
        bed_change = bed_change - morph_factor * (rows_diff(flux_rows) + column_diff(flux_second))
    weight_all = weights.astype(jnp.float32)
    weight_mine = lax.dynamic_slice_in_dim(
        weight_all, lax.axis_index("cond") * cond_here, cond_here
    )
    own_part = jnp.sum(weight_mine[:, None, None] * bed_change, 0) / jnp.sum(weight_all)
    portion = lax.psum(own_part, "cond")
    padded = rim_cells(diffusivity)
    centre = padded[1:-1, 1:-1]
    coefs = [centre * other / (centre + other) for other in neighbours(padded)]
    rhs = bed + portion
    solution = jnp.zeros_like(rhs)
    image = apply_op(rhs, coefs)
    totals = reduce_all(jnp.stack([jnp.sum(rhs * rhs), jnp.sum(rhs * image)]))
    norm_now = totals[0]
    alpha = norm_now / totals[1]
    residual, direction, along = (rhs, rhs, image)
    for sweep in range(ITERS):
        solution = solution + alpha * direction
        if sweep + 1 < ITERS:
            residual = residual - alpha * along
            image = apply_op(residual, coefs)
            totals = reduce_all(
                jnp.stack([jnp.sum(residual * residual), jnp.sum(residual * image)])
            )
            ratio = totals[0] / norm_now
            alpha = totals[0] / (totals[1] - ratio * totals[0] / alpha)
            direction = residual + ratio * direction
            along = image + ratio * along
            norm_now = totals[0]
    return (state_now[:, 0], solution)


def solution(mesh):
    in_specs = (
        P("cond", None, "space", None),
        P("cond", None, "space", None),
        P("cond", "space", None),
        P("space", None),
        P("space", None),
        P(),
        P("space", None),
        P("space", None),
    )
    out_specs = (P("cond", "space", None), P("space", None))
    return jax.shard_map(local, mesh=mesh, in_specs=in_specs, out_specs=out_specs, check_vma=False)
```

profile of v0, /device:TPU:0, one launch (start us, length us, event | category | flops | bytes accessed | tf_op | source)
XLA Modules:
  0.0 204.6 jit_solution(7893001801209511206)
XLA Ops:
  7.2 1.2 fusion.205
  8.4 2.5 %collective-permute-start = (f32[2,2,1,2048]{3,2,0,1:T(1,128)S(1)}, f32[2,2,1,2048]{3,2,0,1:T(1,128)S(1)}, u32[]{:S(2)}, u32[]{:S(2)}) collective-permute-start(f32[2,2,1,2048]{3,2,0,1:T(1,128)S(1)} %get-tuple-element.99), channel_id=1, source_target_pairs={{0,1},{1,2},{2,3},{3,4},{4,5},{5,6},{6,7},{8,9},{9,10},{10,11},{11... | collective-permute-start | bytes 98312 | tf_op jit(solution)/shard_map/ppermute | solution.py:26
  11.0 1.3 collective-permute-start.1
  12.3 3.9 %collective-permute-done.1 = f32[2,2,1,2048]{3,2,0,1:T(1,128)S(1)} collective-permute-done((f32[2,2,1,2048]{3,2,0,1:T(1,128)S(1)}, f32[2,2,1,2048]{3,2,0,1:T(1,128)S(1)}, u32[]{:S(2)}, u32[]{:S(2)}) %collective-permute-start.1) | collective-permute-done | bytes 32800 | tf_op jit(solution)/shard_map/ppermute | solution.py:28
  16.5 1.0 copy-done
  18.3 4.5 %collective-permute-start.2 = (f32[2,2,1,2048]{3,2,0,1:T(1,128)S(1)}, f32[2,2,1,2048]{3,2,0,1:T(1,128)S(1)}, u32[]{:S(2)}, u32[]{:S(2)}) collective-permute-start(f32[2,2,1,2048]{3,2,0,1:T(1,128)S(1)} %get-tuple-element.97), channel_id=1, source_target_pairs={{0,1},{1,2},{2,3},{3,4},{4,5},{5,6},{6,7},{8,9},{9,10},{10,11},{11... | collective-permute-start | bytes 98312 | tf_op jit(solution)/shard_map/ppermute | solution.py:26
  22.9 1.3 collective-permute-start.3
  24.2 1.8 collective-permute-done.3
  27.0 4.1 %collective-permute-start.4 = (f32[2,2,1,2048]{3,2,0,1:T(1,128)S(1)}, f32[2,2,1,2048]{3,2,0,1:T(1,128)S(1)}, u32[]{:S(2)}, u32[]{:S(2)}) collective-permute-start(f32[2,2,1,2048]{3,2,0,1:T(1,128)S(1)} %get-tuple-element.95), channel_id=1, source_target_pairs={{0,1},{1,2},{2,3},{3,4},{4,5},{5,6},{6,7},{8,9},{9,10},{10,11},{11... | collective-permute-start | bytes 98312 | tf_op jit(solution)/shard_map/ppermute | solution.py:26
  31.0 1.3 collective-permute-start.5
  32.4 1.8 collective-permute-done.5
  34.3 0.2 bitcast_multiply_fusion.6
  34.8 0.3 fusion.6
  35.2 4.1 %collective-permute-start.6 = (f32[2,2,1,2048]{3,2,0,1:T(1,128)S(1)}, f32[2,2,1,2048]{3,2,0,1:T(1,128)S(1)}, u32[]{:S(2)}, u32[]{:S(2)}) collective-permute-start(f32[2,2,1,2048]{3,2,0,1:T(1,128)S(1)} %get-tuple-element.93), channel_id=1, source_target_pairs={{0,1},{1,2},{2,3},{3,4},{4,5},{5,6},{6,7},{8,9},{9,10},{10,11},{11... | collective-permute-start | bytes 98312 | tf_op jit(solution)/shard_map/ppermute | solution.py:26
  39.3 1.3 collective-permute-start.7
  40.6 1.8 collective-permute-done.7
  43.0 0.4 fusion.9
  43.6 4.1 %collective-permute-start.8 = (f32[2,2,1,2048]{3,2,0,1:T(1,128)S(1)}, f32[2,2,1,2048]{3,2,0,1:T(1,128)S(1)}, u32[]{:S(2)}, u32[]{:S(2)}) collective-permute-start(f32[2,2,1,2048]{3,2,0,1:T(1,128)S(1)} %get-tuple-element.91), channel_id=1, source_target_pairs={{0,1},{1,2},{2,3},{3,4},{4,5},{5,6},{6,7},{8,9},{9,10},{10,11},{11... | collective-permute-start | bytes 98312 | tf_op jit(solution)/shard_map/ppermute | solution.py:26
  47.6 1.3 collective-permute-start.9
  48.9 1.8 collective-permute-done.9
  50.9 0.3 bitcast_multiply_fusion.3
  51.4 0.5 fusion.11
  52.1 4.1 %collective-permute-start.10 = (f32[2,2,1,2048]{3,2,0,1:T(1,128)S(1)}, f32[2,2,1,2048]{3,2,0,1:T(1,128)S(1)}, u32[]{:S(2)}, u32[]{:S(2)}) collective-permute-start(f32[2,2,1,2048]{3,2,0,1:T(1,128)S(1)} %get-tuple-element.89), channel_id=1, source_target_pairs={{0,1},{1,2},{2,3},{3,4},{4,5},{5,6},{6,7},{8,9},{9,10},{10,11},{11... | collective-permute-start | bytes 98312 | tf_op jit(solution)/shard_map/ppermute | solution.py:26
  56.1 1.3 collective-permute-start.11
  57.5 1.3 collective-permute-start.16
  58.8 3.7 %collective-permute-start.17 = (f32[2,1,2048]{2,1,0:T(1,128)S(1)}, f32[2,1,2048]{2,1,0:T(1,128)S(1)}, u32[]{:S(2)}, u32[]{:S(2)}) collective-permute-start(f32[2,1,2048]{2,1,0:T(1,128)S(1)} %get-tuple-element.102), channel_id=1, source_target_pairs={{0,1},{1,2},{2,3},{3,4},{4,5},{5,6},{6,7},{8,9},{9,10},{10,11},{11... | collective-permute-start | bytes 49160 | tf_op jit(solution)/shard_map/ppermute | solution.py:26
  63.1 0.7 fusion.14
  63.9 3.6 %collective-permute-start.12 = (f32[2,2,1,2048]{3,2,0,1:T(1,128)S(1)}, f32[2,2,1,2048]{3,2,0,1:T(1,128)S(1)}, u32[]{:S(2)}, u32[]{:S(2)}) collective-permute-start(f32[2,2,1,2048]{3,2,0,1:T(1,128)S(1)} %get-tuple-element.87), channel_id=1, source_target_pairs={{0,1},{1,2},{2,3},{3,4},{4,5},{5,6},{6,7},{8,9},{9,10},{10,11},{11... | collective-permute-start | bytes 98312 | tf_op jit(solution)/shard_map/ppermute | solution.py:26
  67.5 1.3 collective-permute-start.13
  68.9 1.3 collective-permute-start.18
  70.2 0.5 collective-permute-done.13
  71.3 0.8 fusion.16
  72.1 4.1 %collective-permute-start.14 = (f32[2,2,1,2048]{3,2,0,1:T(1,128)S(1)}, f32[2,2,1,2048]{3,2,0,1:T(1,128)S(1)}, u32[]{:S(2)}, u32[]{:S(2)}) collective-permute-start(f32[2,2,1,2048]{3,2,0,1:T(1,128)S(1)} %get-tuple-element.85), channel_id=1, source_target_pairs={{0,1},{1,2},{2,3},{3,4},{4,5},{5,6},{6,7},{8,9},{9,10},{10,11},{11... | collective-permute-start | bytes 98312 | tf_op jit(solution)/shard_map/ppermute | solution.py:26
  76.2 1.3 collective-permute-start.15
  77.5 3.4 %collective-permute-start.19 = (f32[2,1,2048]{2,1,0:T(1,128)S(1)}, f32[2,1,2048]{2,1,0:T(1,128)S(1)}, u32[]{:S(2)}, u32[]{:S(2)}) collective-permute-start(f32[2,1,2048]{2,1,0:T(1,128)S(1)} %get-tuple-element.104), channel_id=1, source_target_pairs={{0,1},{1,2},{2,3},{3,4},{4,5},{5,6},{6,7},{8,9},{9,10},{10,11},{11... | collective-permute-start | bytes 49160 | tf_op jit(solution)/shard_map/ppermute | solution.py:26
  81.0 1.3 collective-permute-start.20
  82.9 0.9 fusion.19
  84.0 4.3 %collective-permute-start.21 = (f32[2,1,2048]{2,1,0:T(1,128)S(1)}, f32[2,1,2048]{2,1,0:T(1,128)S(1)}, u32[]{:S(2)}, u32[]{:S(2)}) collective-permute-start(f32[2,1,2048]{2,1,0:T(1,128)S(1)} %get-tuple-element.106), channel_id=1, source_target_pairs={{0,1},{1,2},{2,3},{3,4},{4,5},{5,6},{6,7},{8,9},{9,10},{10,11},{11... | collective-permute-start | bytes 49160 | tf_op jit(solution)/shard_map/ppermute | solution.py:26
  88.3 1.3 collective-permute-start.22
  89.6 4.5 %collective-permute-start.23 = (f32[2,1,2048]{2,1,0:T(1,128)S(1)}, f32[2,1,2048]{2,1,0:T(1,128)S(1)}, u32[]{:S(2)}, u32[]{:S(2)}) collective-permute-start(f32[2,1,2048]{2,1,0:T(1,128)S(1)} %get-tuple-element.108), channel_id=1, source_target_pairs={{0,1},{1,2},{2,3},{3,4},{4,5},{5,6},{6,7},{8,9},{9,10},{10,11},{11... | collective-permute-start | bytes 49160 | tf_op jit(solution)/shard_map/ppermute | solution.py:26
  94.1 0.6 convert_reduce_fusion
  94.8 0.6 fusion.108
  95.4 1.4 broadcast_divide_fusion
  96.8 0.9 copy-done.3
  97.7 3.6 %collective-permute-start.24 = (f32[1,2048]{1,0:T(1,128)S(1)}, f32[1,2048]{1,0:T(1,128)S(1)}, u32[]{:S(2)}, u32[]{:S(2)}) collective-permute-start(f32[1,2048]{1,0:T(1,128)S(1)} %get-tuple-element.111), channel_id=1, source_target_pairs={{0,1},{1,2},{2,3},{3,4},{4,5},{5,6},{6,7},{8,9},{9,10},{10,11},{11... | collective-permute-start | bytes 24584 | tf_op jit(solution)/shard_map/ppermute | solution.py:26
  101.3 1.3 collective-permute-start.26
  102.6 40.1 %all-reduce.25.cloned.1.call-done = f32[16,2048]{1,0:T(8,128)} async-done(((f32[16,2048]{1,0:T(8,128)}), f32[16,2048]{1,0:T(8,128)}) %all-reduce.25.cloned.1.call-update) | async-done | bytes 131088 | tf_op jit(solution)/shard_map/psum | solution.py:115
  142.7 0.9 add.321
  143.7 1.3 collective-permute-start.25
  145.0 1.3 collective-permute-start.27
  146.5 3.3 %collective-permute-done.27 = f32[1,2048]{1,0:T(1,128)S(1)} collective-permute-done((f32[1,2048]{1,0:T(1,128)S(1)}, f32[1,2048]{1,0:T(1,128)S(1)}, u32[]{:S(2)}, u32[]{:S(2)}) %collective-permute-start.27) | collective-permute-done | bytes 8224 | tf_op jit(solution)/shard_map/ppermute | solution.py:28
  149.9 0.9 multiply_reduce_fusion.2
  150.8 1.4 pad_maximum_fusion.38
  152.1 16.0 %psum.22 = f32[2]{0:T(128)S(1)} all-reduce(f32[2]{0:T(128)S(1)} %pad_maximum_fusion.38), channel_id=1, replica_groups=mesh['cond'=4,'space'=8] {'space'}, use_global_device_ids=true, to_apply=%region_5.6 | all-reduce | flops 2 | bytes 16 | tf_op jit(solution)/shard_map/psum | solution.py:84
  168.1 0.6 fusion.214
  170.1 1.3 collective-permute-start.28
  171.4 1.3 collective-permute-start.29
  172.7 1.8 collective-permute-done.29
  174.6 0.9 multiply_reduce_fusion
  175.5 1.4 pad_maximum_fusion.39
  176.9 0.7 slice_bitcast_fusion.18
  177.6 14.5 %psum.23 = f32[2]{0:T(128)S(1)} all-reduce(f32[2]{0:T(128)S(1)} %pad_maximum_fusion.39), channel_id=1, replica_groups=mesh['cond'=4,'space'=8] {'space'}, use_global_device_ids=true, to_apply=%region_8.9 | all-reduce | flops 2 | bytes 16 | tf_op jit(solution)/shard_map/psum | solution.py:84
  192.1 0.7 fusion.213
  197.1 0.7 multiply_add_fusion
  (101 shorter events, 6.6 us)
Async XLA Ops:
  7.2 135.5 %all-reduce.25.cloned.1.call-start = ((), (), s32[]{:S(2)}) async-start(), calls=%async_computation | async-start | bytes 262144 | tf_op jit(solution)/shard_map/psum | solution.py:115
  8.4 3.9 %copy-start.4 = (s32[2,16,2048]{2,1,0:T(8,128)S(1)}, s32[2,16,2048]{2,1,0:T(8,128)}, u32[]{:S(2)}) copy-start(s32[2,16,2048]{2,1,0:T(8,128)} %param.10) | copy-start | bytes 786436
  8.4 3.9 %collective-permute-start = (f32[2,2,1,2048]{3,2,0,1:T(1,128)S(1)}, f32[2,2,1,2048]{3,2,0,1:T(1,128)S(1)}, u32[]{:S(2)}, u32[]{:S(2)}) collective-permute-start(f32[2,2,1,2048]{3,2,0,1:T(1,128)S(1)} %get-tuple-element.99), channel_id=1, source_target_pairs={{0,1},{1,2},{2,3},{3,4},{4,5},{5,6},{6,7},{8,9},{9,10},{10,11},{11... | collective-permute-start | bytes 98312 | tf_op jit(solution)/shard_map/ppermute | solution.py:26
  11.0 5.3 %collective-permute-start.1 = (f32[2,2,1,2048]{3,2,0,1:T(1,128)S(1)}, f32[2,2,1,2048]{3,2,0,1:T(1,128)S(1)}, u32[]{:S(2)}, u32[]{:S(2)}) collective-permute-start(f32[2,2,1,2048]{3,2,0,1:T(1,128)S(1)} %get-tuple-element.100), channel_id=1, source_target_pairs={{1,0},{2,1},{3,2},{4,3},{5,4},{6,5},{7,6},{9,8},{10,9},{11,10},{12... | collective-permute-start | bytes 98312 | tf_op jit(solution)/shard_map/ppermute | solution.py:28
  16.4 1.1 copy-start
  16.4 1.3 copy-start.1
  16.4 1.3 copy-start.2
  18.3 5.8 %collective-permute-start.2 = (f32[2,2,1,2048]{3,2,0,1:T(1,128)S(1)}, f32[2,2,1,2048]{3,2,0,1:T(1,128)S(1)}, u32[]{:S(2)}, u32[]{:S(2)}) collective-permute-start(f32[2,2,1,2048]{3,2,0,1:T(1,128)S(1)} %get-tuple-element.97), channel_id=1, source_target_pairs={{0,1},{1,2},{2,3},{3,4},{4,5},{5,6},{6,7},{8,9},{9,10},{10,11},{11... | collective-permute-start | bytes 98312 | tf_op jit(solution)/shard_map/ppermute | solution.py:26
  22.9 3.1 %collective-permute-start.3 = (f32[2,2,1,2048]{3,2,0,1:T(1,128)S(1)}, f32[2,2,1,2048]{3,2,0,1:T(1,128)S(1)}, u32[]{:S(2)}, u32[]{:S(2)}) collective-permute-start(f32[2,2,1,2048]{3,2,0,1:T(1,128)S(1)} %get-tuple-element.98), channel_id=1, source_target_pairs={{1,0},{2,1},{3,2},{4,3},{5,4},{6,5},{7,6},{9,8},{10,9},{11,10},{12... | collective-permute-start | bytes 98312 | tf_op jit(solution)/shard_map/ppermute | solution.py:28
  26.9 5.4 %copy-start.6 = (s32[16,2048]{1,0:T(8,128)S(1)}, s32[16,2048]{1,0:T(8,128)}, u32[]{:S(2)}) copy-start(s32[16,2048]{1,0:T(8,128)} %param.12) | copy-start | bytes 393220
  27.0 5.4 %collective-permute-start.4 = (f32[2,2,1,2048]{3,2,0,1:T(1,128)S(1)}, f32[2,2,1,2048]{3,2,0,1:T(1,128)S(1)}, u32[]{:S(2)}, u32[]{:S(2)}) collective-permute-start(f32[2,2,1,2048]{3,2,0,1:T(1,128)S(1)} %get-tuple-element.95), channel_id=1, source_target_pairs={{0,1},{1,2},{2,3},{3,4},{4,5},{5,6},{6,7},{8,9},{9,10},{10,11},{11... | collective-permute-start | bytes 98312 | tf_op jit(solution)/shard_map/ppermute | solution.py:26
  31.0 3.1 %collective-permute-start.5 = (f32[2,2,1,2048]{3,2,0,1:T(1,128)S(1)}, f32[2,2,1,2048]{3,2,0,1:T(1,128)S(1)}, u32[]{:S(2)}, u32[]{:S(2)}) collective-permute-start(f32[2,2,1,2048]{3,2,0,1:T(1,128)S(1)} %get-tuple-element.96), channel_id=1, source_target_pairs={{1,0},{2,1},{3,2},{4,3},{5,4},{6,5},{7,6},{9,8},{10,9},{11,10},{12... | collective-permute-start | bytes 98312 | tf_op jit(solution)/shard_map/ppermute | solution.py:28
  35.2 5.4 %collective-permute-start.6 = (f32[2,2,1,2048]{3,2,0,1:T(1,128)S(1)}, f32[2,2,1,2048]{3,2,0,1:T(1,128)S(1)}, u32[]{:S(2)}, u32[]{:S(2)}) collective-permute-start(f32[2,2,1,2048]{3,2,0,1:T(1,128)S(1)} %get-tuple-element.93), channel_id=1, source_target_pairs={{0,1},{1,2},{2,3},{3,4},{4,5},{5,6},{6,7},{8,9},{9,10},{10,11},{11... | collective-permute-start | bytes 98312 | tf_op jit(solution)/shard_map/ppermute | solution.py:26
  39.3 3.1 %collective-permute-start.7 = (f32[2,2,1,2048]{3,2,0,1:T(1,128)S(1)}, f32[2,2,1,2048]{3,2,0,1:T(1,128)S(1)}, u32[]{:S(2)}, u32[]{:S(2)}) collective-permute-start(f32[2,2,1,2048]{3,2,0,1:T(1,128)S(1)} %get-tuple-element.94), channel_id=1, source_target_pairs={{1,0},{2,1},{3,2},{4,3},{5,4},{6,5},{7,6},{9,8},{10,9},{11,10},{12... | collective-permute-start | bytes 98312 | tf_op jit(solution)/shard_map/ppermute | solution.py:28
  43.6 5.4 %collective-permute-start.8 = (f32[2,2,1,2048]{3,2,0,1:T(1,128)S(1)}, f32[2,2,1,2048]{3,2,0,1:T(1,128)S(1)}, u32[]{:S(2)}, u32[]{:S(2)}) collective-permute-start(f32[2,2,1,2048]{3,2,0,1:T(1,128)S(1)} %get-tuple-element.91), channel_id=1, source_target_pairs={{0,1},{1,2},{2,3},{3,4},{4,5},{5,6},{6,7},{8,9},{9,10},{10,11},{11... | collective-permute-start | bytes 98312 | tf_op jit(solution)/shard_map/ppermute | solution.py:26
  47.6 3.1 %collective-permute-start.9 = (f32[2,2,1,2048]{3,2,0,1:T(1,128)S(1)}, f32[2,2,1,2048]{3,2,0,1:T(1,128)S(1)}, u32[]{:S(2)}, u32[]{:S(2)}) collective-permute-start(f32[2,2,1,2048]{3,2,0,1:T(1,128)S(1)} %get-tuple-element.92), channel_id=1, source_target_pairs={{1,0},{2,1},{3,2},{4,3},{5,4},{6,5},{7,6},{9,8},{10,9},{11,10},{12... | collective-permute-start | bytes 98312 | tf_op jit(solution)/shard_map/ppermute | solution.py:28
  52.1 10.4 %collective-permute-start.10 = (f32[2,2,1,2048]{3,2,0,1:T(1,128)S(1)}, f32[2,2,1,2048]{3,2,0,1:T(1,128)S(1)}, u32[]{:S(2)}, u32[]{:S(2)}) collective-permute-start(f32[2,2,1,2048]{3,2,0,1:T(1,128)S(1)} %get-tuple-element.89), channel_id=1, source_target_pairs={{0,1},{1,2},{2,3},{3,4},{4,5},{5,6},{6,7},{8,9},{9,10},{10,11},{11... | collective-permute-start | bytes 98312 | tf_op jit(solution)/shard_map/ppermute | solution.py:26
  56.1 6.3 %collective-permute-start.11 = (f32[2,2,1,2048]{3,2,0,1:T(1,128)S(1)}, f32[2,2,1,2048]{3,2,0,1:T(1,128)S(1)}, u32[]{:S(2)}, u32[]{:S(2)}) collective-permute-start(f32[2,2,1,2048]{3,2,0,1:T(1,128)S(1)} %get-tuple-element.90), channel_id=1, source_target_pairs={{1,0},{2,1},{3,2},{4,3},{5,4},{6,5},{7,6},{9,8},{10,9},{11,10},{12... | collective-permute-start | bytes 98312 | tf_op jit(solution)/shard_map/ppermute | solution.py:28
  57.5 26.5 %collective-permute-start.16 = (f32[2,1,2048]{2,1,0:T(1,128)S(1)}, f32[2,1,2048]{2,1,0:T(1,128)S(1)}, u32[]{:S(2)}, u32[]{:S(2)}) collective-permute-start(f32[2,1,2048]{2,1,0:T(1,128)S(1)} %get-tuple-element.101), channel_id=1, source_target_pairs={{1,0},{2,1},{3,2},{4,3},{5,4},{6,5},{7,6},{9,8},{10,9},{11,10},{12... | collective-permute-start | bytes 49160 | tf_op jit(solution)/shard_map/ppermute | solution.py:28
  58.8 29.5 %collective-permute-start.17 = (f32[2,1,2048]{2,1,0:T(1,128)S(1)}, f32[2,1,2048]{2,1,0:T(1,128)S(1)}, u32[]{:S(2)}, u32[]{:S(2)}) collective-permute-start(f32[2,1,2048]{2,1,0:T(1,128)S(1)} %get-tuple-element.102), channel_id=1, source_target_pairs={{0,1},{1,2},{2,3},{3,4},{4,5},{5,6},{6,7},{8,9},{9,10},{10,11},{11... | collective-permute-start | bytes 49160 | tf_op jit(solution)/shard_map/ppermute | solution.py:26
  63.9 6.3 %collective-permute-start.12 = (f32[2,2,1,2048]{3,2,0,1:T(1,128)S(1)}, f32[2,2,1,2048]{3,2,0,1:T(1,128)S(1)}, u32[]{:S(2)}, u32[]{:S(2)}) collective-permute-start(f32[2,2,1,2048]{3,2,0,1:T(1,128)S(1)} %get-tuple-element.87), channel_id=1, source_target_pairs={{0,1},{1,2},{2,3},{3,4},{4,5},{5,6},{6,7},{8,9},{9,10},{10,11},{11... | collective-permute-start | bytes 98312 | tf_op jit(solution)/shard_map/ppermute | solution.py:26
  67.5 3.1 %collective-permute-start.13 = (f32[2,2,1,2048]{3,2,0,1:T(1,128)S(1)}, f32[2,2,1,2048]{3,2,0,1:T(1,128)S(1)}, u32[]{:S(2)}, u32[]{:S(2)}) collective-permute-start(f32[2,2,1,2048]{3,2,0,1:T(1,128)S(1)} %get-tuple-element.88), channel_id=1, source_target_pairs={{1,0},{2,1},{3,2},{4,3},{5,4},{6,5},{7,6},{9,8},{10,9},{11,10},{12... | collective-permute-start | bytes 98312 | tf_op jit(solution)/shard_map/ppermute | solution.py:28
  68.9 20.7 %collective-permute-start.18 = (f32[2,1,2048]{2,1,0:T(1,128)S(1)}, f32[2,1,2048]{2,1,0:T(1,128)S(1)}, u32[]{:S(2)}, u32[]{:S(2)}) collective-permute-start(f32[2,1,2048]{2,1,0:T(1,128)S(1)} %get-tuple-element.103), channel_id=1, source_target_pairs={{1,0},{2,1},{3,2},{4,3},{5,4},{6,5},{7,6},{9,8},{10,9},{11,10},{12... | collective-permute-start | bytes 49160 | tf_op jit(solution)/shard_map/ppermute | solution.py:28
  72.1 5.4 %collective-permute-start.14 = (f32[2,2,1,2048]{3,2,0,1:T(1,128)S(1)}, f32[2,2,1,2048]{3,2,0,1:T(1,128)S(1)}, u32[]{:S(2)}, u32[]{:S(2)}) collective-permute-start(f32[2,2,1,2048]{3,2,0,1:T(1,128)S(1)} %get-tuple-element.85), channel_id=1, source_target_pairs={{0,1},{1,2},{2,3},{3,4},{4,5},{5,6},{6,7},{8,9},{9,10},{10,11},{11... | collective-permute-start | bytes 98312 | tf_op jit(solution)/shard_map/ppermute | solution.py:26
  76.2 4.8 %collective-permute-start.15 = (f32[2,2,1,2048]{3,2,0,1:T(1,128)S(1)}, f32[2,2,1,2048]{3,2,0,1:T(1,128)S(1)}, u32[]{:S(2)}, u32[]{:S(2)}) collective-permute-start(f32[2,2,1,2048]{3,2,0,1:T(1,128)S(1)} %get-tuple-element.86), channel_id=1, source_target_pairs={{1,0},{2,1},{3,2},{4,3},{5,4},{6,5},{7,6},{9,8},{10,9},{11,10},{12... | collective-permute-start | bytes 98312 | tf_op jit(solution)/shard_map/ppermute | solution.py:28
  77.5 17.2 %collective-permute-start.19 = (f32[2,1,2048]{2,1,0:T(1,128)S(1)}, f32[2,1,2048]{2,1,0:T(1,128)S(1)}, u32[]{:S(2)}, u32[]{:S(2)}) collective-permute-start(f32[2,1,2048]{2,1,0:T(1,128)S(1)} %get-tuple-element.104), channel_id=1, source_target_pairs={{0,1},{1,2},{2,3},{3,4},{4,5},{5,6},{6,7},{8,9},{9,10},{10,11},{11... | collective-permute-start | bytes 49160 | tf_op jit(solution)/shard_map/ppermute | solution.py:26
  81.0 13.8 %collective-permute-start.20 = (f32[2,1,2048]{2,1,0:T(1,128)S(1)}, f32[2,1,2048]{2,1,0:T(1,128)S(1)}, u32[]{:S(2)}, u32[]{:S(2)}) collective-permute-start(f32[2,1,2048]{2,1,0:T(1,128)S(1)} %get-tuple-element.105), channel_id=1, source_target_pairs={{1,0},{2,1},{3,2},{4,3},{5,4},{6,5},{7,6},{9,8},{10,9},{11,10},{12... | collective-permute-start | bytes 49160 | tf_op jit(solution)/shard_map/ppermute | solution.py:28
  84.0 10.8 %collective-permute-start.21 = (f32[2,1,2048]{2,1,0:T(1,128)S(1)}, f32[2,1,2048]{2,1,0:T(1,128)S(1)}, u32[]{:S(2)}, u32[]{:S(2)}) collective-permute-start(f32[2,1,2048]{2,1,0:T(1,128)S(1)} %get-tuple-element.106), channel_id=1, source_target_pairs={{0,1},{1,2},{2,3},{3,4},{4,5},{5,6},{6,7},{8,9},{9,10},{10,11},{11... | collective-permute-start | bytes 49160 | tf_op jit(solution)/shard_map/ppermute | solution.py:26
  88.3 5.8 %copy-start.7 = (s32[8]{0:T(128)S(1)}, s32[8]{0:T(128)}, u32[]{:S(2)}) copy-start(s32[8]{0:T(128)} %param.13) | copy-start | bytes 100
  88.3 6.5 %collective-permute-start.22 = (f32[2,1,2048]{2,1,0:T(1,128)S(1)}, f32[2,1,2048]{2,1,0:T(1,128)S(1)}, u32[]{:S(2)}, u32[]{:S(2)}) collective-permute-start(f32[2,1,2048]{2,1,0:T(1,128)S(1)} %get-tuple-element.107), channel_id=1, source_target_pairs={{1,0},{2,1},{3,2},{4,3},{5,4},{6,5},{7,6},{9,8},{10,9},{11,10},{12... | collective-permute-start | bytes 49160 | tf_op jit(solution)/shard_map/ppermute | solution.py:28
  89.6 5.2 %collective-permute-start.23 = (f32[2,1,2048]{2,1,0:T(1,128)S(1)}, f32[2,1,2048]{2,1,0:T(1,128)S(1)}, u32[]{:S(2)}, u32[]{:S(2)}) collective-permute-start(f32[2,1,2048]{2,1,0:T(1,128)S(1)} %get-tuple-element.108), channel_id=1, source_target_pairs={{0,1},{1,2},{2,3},{3,4},{4,5},{5,6},{6,7},{8,9},{9,10},{10,11},{11... | collective-permute-start | bytes 49160 | tf_op jit(solution)/shard_map/ppermute | solution.py:26
  95.4 47.3 %copy-start.5 = (f32[16,2048]{1,0:T(8,128)S(1)}, f32[16,2048]{1,0:T(8,128)}, u32[]{:S(2)}) copy-start(f32[16,2048]{1,0:T(8,128)} %param.14) | copy-start | bytes 393220
  96.8 0.9 copy-start.3
  97.7 48.6 %collective-permute-start.24 = (f32[1,2048]{1,0:T(1,128)S(1)}, f32[1,2048]{1,0:T(1,128)S(1)}, u32[]{:S(2)}, u32[]{:S(2)}) collective-permute-start(f32[1,2048]{1,0:T(1,128)S(1)} %get-tuple-element.111), channel_id=1, source_target_pairs={{0,1},{1,2},{2,3},{3,4},{4,5},{5,6},{6,7},{8,9},{9,10},{10,11},{11... | collective-permute-start | bytes 24584 | tf_op jit(solution)/shard_map/ppermute | solution.py:26
  101.3 44.9 %collective-permute-start.26 = (f32[1,2048]{1,0:T(1,128)S(1)}, f32[1,2048]{1,0:T(1,128)S(1)}, u32[]{:S(2)}, u32[]{:S(2)}) collective-permute-start(f32[1,2048]{1,0:T(1,128)S(1)} %get-tuple-element.112), channel_id=1, source_target_pairs={{1,0},{2,1},{3,2},{4,3},{5,4},{6,5},{7,6},{9,8},{10,9},{11,10},{12... | collective-permute-start | bytes 24584 | tf_op jit(solution)/shard_map/ppermute | solution.py:28
  143.7 2.8 %collective-permute-start.25 = (f32[1,2048]{1,0:T(1,128)S(1)}, f32[1,2048]{1,0:T(1,128)S(1)}, u32[]{:S(2)}, u32[]{:S(2)}) collective-permute-start(f32[1,2048]{1,0:T(1,128)S(1)} %get-tuple-element.113), channel_id=1, source_target_pairs={{0,1},{1,2},{2,3},{3,4},{4,5},{5,6},{6,7},{8,9},{9,10},{10,11},{11... | collective-permute-start | bytes 24584 | tf_op jit(solution)/shard_map/ppermute | solution.py:26
  145.0 4.8 %collective-permute-start.27 = (f32[1,2048]{1,0:T(1,128)S(1)}, f32[1,2048]{1,0:T(1,128)S(1)}, u32[]{:S(2)}, u32[]{:S(2)}) collective-permute-start(f32[1,2048]{1,0:T(1,128)S(1)} %get-tuple-element.114), channel_id=1, source_target_pairs={{1,0},{2,1},{3,2},{4,3},{5,4},{6,5},{7,6},{9,8},{10,9},{11,10},{12... | collective-permute-start | bytes 24584 | tf_op jit(solution)/shard_map/ppermute | solution.py:28
  170.1 2.6 %collective-permute-start.28 = (f32[1,2048]{1,0:T(1,128)S(1)}, f32[1,2048]{1,0:T(1,128)S(1)}, u32[]{:S(2)}, u32[]{:S(2)}) collective-permute-start(f32[1,2048]{1,0:T(1,128)S(1)} %get-tuple-element.109), channel_id=1, source_target_pairs={{0,1},{1,2},{2,3},{3,4},{4,5},{5,6},{6,7},{8,9},{9,10},{10,11},{11... | collective-permute-start | bytes 24584 | tf_op jit(solution)/shard_map/ppermute | solution.py:26
  171.4 3.1 %collective-permute-start.29 = (f32[1,2048]{1,0:T(1,128)S(1)}, f32[1,2048]{1,0:T(1,128)S(1)}, u32[]{:S(2)}, u32[]{:S(2)}) collective-permute-start(f32[1,2048]{1,0:T(1,128)S(1)} %get-tuple-element.110), channel_id=1, source_target_pairs={{1,0},{2,1},{3,2},{4,3},{5,4},{6,5},{7,6},{9,8},{10,9},{11,10},{12... | collective-permute-start | bytes 24584 | tf_op jit(solution)/shard_map/ppermute | solution.py:28
Sparse Core Ops, SparseCore 0:
  96.9 45.7 all-reduce.24
where the time goes:
time: 206 us; the launch traced here: 205 us
  starting transfers between devices  72.4 us (35%)
  waiting for transfers between devices  56.7 us (28%)
  blocking collectives  30.5 us (15%)
  between operations  20.6 us (10%)
  other arithmetic  19.7 us (10%)
  local copies, waits for them, and re-layouts  4.73 us (2%)
    ppermute x15, starting transfers between devices, with_halo(): lax.ppermute(tail, axis, [(i, (i + 1) % count) for i in range(ends)])  53 us
    psum x1, waiting for transfers between devices, local(): portion = lax.psum(own_part, 'cond')  40.1 us
    psum x2, blocking collectives, reduce_all(): return lax.psum(values, 'space')  30.5 us
    ppermute x15, starting transfers between devices, with_halo(): lax.ppermute(head, axis, [((i + 1) % count, i) for i in range(ends)])  19.4 us
    ppermute x15, waiting for transfers between devices, with_halo(): lax.ppermute(head, axis, [((i + 1) % count, i) for i in range(ends)])  16.6 us
  transfers between devices with their start and end apart: 31, of which 9 were waited for; matrix products, arithmetic and copies ran while one was open for 3% of the time, Pallas kernels for 0%

commit v1 on v0

v1 whole, which is shorter than its diff:
```python
import functools

import jax
import jax.numpy as jnp
from jax import lax
from jax.experimental import pallas as pl
from jax.experimental.pallas import tpu as pltpu
from jax.sharding import PartitionSpec as P

STEPS = 4

time_step = 0.4
gravity = 1.0
friction = 0.1
transport_base = 0.5
morph_factor = 1.0
slope_coeff = 1.0

LANES = 128
ABOVE, BELOW = 1, 2
DEEP = 2 * STEPS + BELOW + 1
NEXT = DEEP - 1
OWN = 24
FLUX_ROWS = BELOW + 1

FLOW = ("elev", "first", "second", "force_a", "force_b", "wet")
HALO = dict(
    elev=DEEP, first=DEEP, depth=DEEP, second=NEXT, force_a=NEXT, force_b=NEXT, wet=NEXT,
    limiter=FLUX_ROWS, bed=BELOW, diffusivity=BELOW,
)
MESSAGE = (FLOW + ("depth", "limiter"), FLOW + ("bed", "diffusivity"))


def offsets(names, tiles):
    places, at = {}, 0
    for name in names:
        places[name] = at
        at += tiles * HALO[name]
    return places, at


def lanes_of(tile):
    return pl.ds(pl.multiple_of(tile * LANES, LANES), LANES)


def own_rows(refs, name, rows, tile):
    if name in ("elev", "first", "second"):
        return refs["flow"][0, ("elev", "first", "second").index(name), rows, lanes_of(tile)]
    if name in ("force_a", "force_b"):
        return refs["forcing"][0, ("force_a", "force_b").index(name), rows, lanes_of(tile)]
    if name == "wet":
        return refs["wet"][0, rows, lanes_of(tile)].astype(jnp.float32)
    return refs[name][rows, lanes_of(tile)].astype(jnp.float32)


def pack_kernel(names, keys, place_ref, *args):
    refs, (across_ref, chip_ref) = dict(zip(keys, args)), args[len(keys) :]
    height, tiles = refs[keys[-1]].shape[-2], refs[keys[-1]].shape[-1] // LANES
    places, _ = offsets(names, tiles)

    def fill(head_ref, tail_ref):
        def body(tile, carry):
            for name in names:
                count = HALO[name]
                where = pl.ds(places[name] + tile * count, count)
                head_ref[where, :] = own_rows(refs, name, slice(0, count), tile)
                tail_ref[where, :] = own_rows(refs, name, slice(height - count, height), tile)
            return carry

        lax.fori_loop(0, tiles, body, 0)

    odd = place_ref[1]

    @pl.when(odd == 0)
    def _():
        fill(across_ref, chip_ref)

    @pl.when(odd == 1)
    def _():
        fill(chip_ref, across_ref)


def beside(field, tile, rows, centre):
    lane = lax.broadcasted_iota(jnp.int32, centre.shape, 1)
    left = pltpu.roll(jnp.where(lane == LANES - 1, field[tile - 1, rows, :], centre), 1, 1)
    right = pltpu.roll(jnp.where(lane == 0, field[tile + 1, rows, :], centre), LANES - 1, 1)
    return left, right


def spread(dst, name, tile, own, head, tail, places, height, base):
    count = HALO[name]
    where = pl.ds(places[name] + tile * count, count)
    dst[tile + 1, base - count : base, :] = head[where, :]
    for row in range(0, height, 8):
        dst[tile + 1, base + row : base + row + 8, :] = own_rows(own, name, slice(row, row + 8), tile)
    dst[tile + 1, base + height : base + height + count, :] = tail[where, :]


def flow_kernel(which, keys, place_ref, weights_ref, *args):
    refs = dict(zip(keys, args))
    n_in = len(keys)
    surface_ref, low_ref, high_ref = args[n_in : n_in + 3]
    names = ("elev", "first", "second", "elev1", "first1", "second1", "wet", "keep", "depth_wet",
             "force_a", "force_b", "depth", "limiter", "flux_a", "flux_b")
    buf = dict(zip(names, args[n_in + 3 :]))
    height, tiles = refs["depth"].shape[0], refs["depth"].shape[1] // LANES
    flow_places, _ = offsets(MESSAGE[which], tiles)
    static_places, _ = offsets(MESSAGE[0], tiles)
    span = buf["elev"].shape[1]

    for name in ("elev", "second", "elev1", "second1", "flux_b"):
        zero = jnp.zeros((span, LANES), jnp.float32)
        buf[name][0, :, :] = zero
        buf[name][tiles + 1, :, :] = zero

    first_tile = (OWN - DEEP) // 8
    last_tile = -(-(OWN + height + DEEP) // 8)

    def load(head, tail, static_head, static_tail):
        def body(tile, carry):
            for name in FLOW:
                spread(buf[name], name, tile, refs, head, tail, flow_places, height, OWN)
            for name in ("depth", "limiter"):
                spread(buf[name], name, tile, refs, static_head, static_tail, static_places, height, OWN)
            at = tile + 1
            for row in range(8 * first_tile, 8 * last_tile, 8):
                rows = slice(row, row + 8)
                wet, depth = buf["wet"][at, rows, :], buf["depth"][at, rows, :]
                half = (0.5 * time_step) * wet
                depth_wet = depth * half
                buf["first"][at, rows, :] = depth * buf["first"][at, rows, :]
                buf["second"][at, rows, :] = depth * buf["second"][at, rows, :]
                buf["force_a"][at, rows, :] = 2.0 * depth_wet * buf["force_a"][at, rows, :]
                buf["force_b"][at, rows, :] = 2.0 * depth_wet * buf["force_b"][at, rows, :]
                buf["wet"][at, rows, :] = half
                buf["keep"][at, rows, :] = 1.0 - (2.0 * friction) * half
                buf["depth_wet"][at, rows, :] = gravity * depth_wet
                buf["depth"][at, rows, :] = jnp.where(depth > 0.0, 1.0 / depth, 0.0)
            return carry

        lax.fori_loop(0, tiles, body, 0)

    odd = place_ref[1]

    @pl.when(odd == 0)
    def _():
        load(refs["across"], refs["chip"], refs["static_across"], refs["static_chip"])

    @pl.when(odd == 1)
    def _():
        load(refs["chip"], refs["across"], refs["static_chip"], refs["static_across"])

    def section(number):
        second = number % 2 == 0
        source = ("elev1", "first1", "second1") if second else ("elev", "first", "second")
        target = ("elev", "first", "second") if second else ("elev1", "first1", "second1")
        elev, first, vert = (buf[name] for name in source)
        begin = (OWN - DEEP + 1 + number) // 8
        end = -(-(OWN + height + DEEP - number) // 8)
        flux_begin = (OWN - FLUX_ROWS + 1) // 8
        flux_end = -(-(OWN + height + FLUX_ROWS) // 8)
        last = number == 2 * STEPS

        def body(tile, carry):
            at = tile + 1
            for block in range(begin, end):
                row = 8 * block
                rows, up, down = slice(row, row + 8), slice(row - 1, row + 7), slice(row + 1, row + 9)
                e, f, s = elev[at, rows, :], first[at, rows, :], vert[at, rows, :]
                e_left, e_right = beside(elev, at, rows, e)
                s_left, s_right = beside(vert, at, rows, s)
                keep, depth_wet = buf["keep"][at, rows, :], buf["depth_wet"][at, rows, :]
                gone = (first[at, down, :] - first[at, up, :]) + (s_right - s_left)
                new_e = e - buf["wet"][at, rows, :] * gone
                new_f = (keep * f + buf["force_a"][at, rows, :]) - depth_wet * (elev[at, down, :] - elev[at, up, :])
                new_s = (keep * s + buf["force_b"][at, rows, :]) - depth_wet * (e_right - e_left)
                if second:
                    new_e = 0.5 * (buf["elev"][at, rows, :] + new_e)
                    new_f = 0.5 * (buf["first"][at, rows, :] + new_f)
                    new_s = 0.5 * (buf["second"][at, rows, :] + new_s)
                if not last:
                    buf[target[0]][at, rows, :] = new_e
                    buf[target[1]][at, rows, :] = new_f
                    buf[target[2]][at, rows, :] = new_s
                elif 0 <= row - OWN < height:
                    surface_ref[0, row - OWN : row - OWN + 8, lanes_of(tile)] = new_e
                if second and flux_begin <= block < flux_end:
                    inverse = buf["depth"][at, rows, :]
                    vel_a, vel_b = new_f * inverse, new_s * inverse
                    energy = vel_a * vel_a + vel_b * vel_b
                    factor = (transport_base + energy) / (1.0 + buf["limiter"][at, rows, :] * energy)
                    flux_a, flux_b = vel_a * factor, vel_b * factor
                    if number > 2:
                        flux_a = buf["flux_a"][at, rows, :] + flux_a
                        flux_b = buf["flux_b"][at, rows, :] + flux_b
                    buf["flux_a"][at, rows, :] = flux_a
                    buf["flux_b"][at, rows, :] = flux_b
            return carry

        lax.fori_loop(0, tiles, body, 0)

    for number in range(1, 2 * STEPS + 1):
        section(number)

    total = weights_ref[0]
    for other in range(1, weights_ref.shape[0]):
        total = total + weights_ref[other]
    scale = jnp.full((8, LANES), weights_ref[place_ref[0] + which], jnp.int32).astype(jnp.float32)
    scale = (-0.5 * morph_factor) * scale / jnp.full((8, LANES), total, jnp.int32).astype(jnp.float32)
    reach = height + ABOVE + BELOW
    begins = list(range(0, reach - 7, 8))
    if begins[-1] + 8 < reach:
        begins.append(reach - 8)

    def emit(out_ref, before, start):
        def body(local_tile, carry):
            at = start + local_tile + 1
            for begin in begins:
                row = OWN - ABOVE + begin
                rows, up, down = slice(row, row + 8), slice(row - 1, row + 7), slice(row + 1, row + 9)
                flux_b = buf["flux_b"][at, rows, :]
                left, right = beside(buf["flux_b"], at, rows, flux_b)
                change = (buf["flux_a"][at, down, :] - buf["flux_a"][at, up, :]) + (right - left)
                where = pl.ds(local_tile * reach + begin, 8)
                piece = scale * change
                if before is not None:
                    piece = before[where, :] + piece
                out_ref[where, :] = piece
            return carry

        lax.fori_loop(0, tiles // 2, body, 0)

    emit(low_ref, refs.get("low"), 0)
    emit(high_ref, refs.get("high"), tiles // 2)


def moment_kernel(keys, place_ref, *args):
    refs = dict(zip(keys, args))
    n_in = len(keys)
    rhs_ref, image_ref, moments_ref, field, diffuse, image, down_k, right_k = args[n_in:]
    height, tiles = refs["bed"].shape[0], refs["bed"].shape[1] // LANES
    places, _ = offsets(MESSAGE[1], tiles)
    base = 8
    reach = height + ABOVE + BELOW
    span = field.shape[1]
    for scratch in (field, diffuse, image):
        zero = jnp.zeros((span, LANES), jnp.float32)
        scratch[0, :, :] = zero
        scratch[tiles + 1, :, :] = zero

    def load(head, tail):
        def fill(tile, carry):
            spread(field, "bed", tile, refs, head, tail, places, height, base)
            spread(diffuse, "diffusivity", tile, refs, head, tail, places, height, base)
            return carry

        lax.fori_loop(0, tiles, fill, 0)

    odd = place_ref[1]

    @pl.when(odd == 0)
    def _():
        load(refs["across"], refs["chip"])

    @pl.when(odd == 1)
    def _():
        load(refs["chip"], refs["across"])

    def add(mine, other, start):
        def body(local_tile, carry):
            where = pl.ds(local_tile * reach, reach)
            rows = slice(base - ABOVE, base - ABOVE + reach)
            at = start + local_tile + 1
            field[at, rows, :] = field[at, rows, :] + (mine[where, :] + other[where, :])
            return carry

        lax.fori_loop(0, tiles // 2, body, 0)

    add(refs["low"], refs["low_other"], 0)
    add(refs["high"], refs["high_other"], tiles // 2)

    def face(here, there):
        both = here + there
        return jnp.where(both > 0.0, slope_coeff * here * there / both, 0.0)

    def apply(tile, carry):
        at = tile + 1
        square, first = carry
        for row in range(base, base + height + 8, 8):
            rows, up, down = slice(row, row + 8), slice(row - 1, row + 7), slice(row + 1, row + 9)
            d, x = diffuse[at, rows, :], field[at, rows, :]
            d_left, d_right = beside(diffuse, at, rows, d)
            x_left, x_right = beside(field, at, rows, x)
            k_down, k_right = face(d, diffuse[at, down, :]), face(d, d_right)
            gap_down, gap_right = x - field[at, down, :], x - x_right
            flow_down, flow_right = k_down * gap_down, k_right * gap_right
            result = (flow_down + face(d, diffuse[at, up, :]) * (x - field[at, up, :])) + (
                flow_right + face(d, d_left) * (x - x_left)
            )
            image[at, rows, :] = result
            down_k[at, rows, :] = k_down
            right_k[at, rows, :] = k_right
            if row < base + height:
                rhs_ref[tile, row - base : row - base + 8, :] = x
                image_ref[tile, row - base : row - base + 8, :] = result
                square = square + x * x
                first = first + (flow_down * gap_down + flow_right * gap_right)
        return square, first

    zero = jnp.zeros((8, LANES), jnp.float32)
    square, first = lax.fori_loop(0, tiles, apply, (zero, zero))

    def again(tile, carry):
        at = tile + 1
        second, third = carry
        lane = lax.broadcasted_iota(jnp.int32, (8, LANES), 1)
        for row in range(base, base + height, 8):
            rows, down = slice(row, row + 8), slice(row + 1, row + 9)
            w = image[at, rows, :]
            w_right = pltpu.roll(jnp.where(lane == 0, image[at + 1, rows, :], w), LANES - 1, 1)
            gap_down, gap_right = w - image[at, down, :], w - w_right
            second = second + w * w
            third = third + (
                down_k[at, rows, :] * gap_down * gap_down + right_k[at, rows, :] * gap_right * gap_right
            )
        return second, third

    second, third = lax.fori_loop(0, tiles, again, (zero, zero))
    for slot, value in enumerate((square, first, second, third)):
        moments_ref[slot : slot + 1, :] = jnp.sum(value, axis=0, keepdims=True)
    moments_ref[4:8, :] = jnp.zeros((4, LANES), jnp.float32)


def final_kernel(rhs_ref, image_ref, *args):
    moments, (out_ref,) = args[:-1], args[-1:]
    total = moments[0][...]
    for part in moments[1:]:
        total = total + part[...]
    total = jnp.sum(total, axis=1, keepdims=True)
    norm, first, second, third = (total[slot : slot + 1, :] for slot in range(4))
    alpha = norm / (norm + first)
    theta = first / norm
    spread_ = second - theta * first
    curve = third - 2.0 * theta * second + theta * theta * first
    ratio = alpha * alpha * spread_ / norm
    beta = spread_ / (spread_ + curve - alpha * spread_ * (spread_ / norm))
    on_rhs = jnp.broadcast_to(alpha + beta * (alpha * theta + ratio), (8, LANES))
    on_image = jnp.broadcast_to(beta * alpha, (8, LANES))
    tiles, height = rhs_ref.shape[:2]

    def body(tile, carry):
        for row in range(0, height, 8):
            rows = slice(row, row + 8)
            out_ref[rows, lanes_of(tile)] = on_rhs * rhs_ref[tile, rows, :] - on_image * image_ref[tile, rows, :]
        return carry

    lax.fori_loop(0, tiles, body, 0)


def whole(shape):
    return pl.BlockSpec(shape, lambda *_: (0,) * len(shape))


def picked(shape, which):
    return pl.BlockSpec((1,) + shape[1:], lambda *_: (which,) + (0,) * (len(shape) - 1))


SMEM = pl.BlockSpec(memory_space=pltpu.SMEM)
PARAMS = dict(vmem_limit_bytes=48 * 1024 * 1024)


def cost(flops, moved):
    return pl.CostEstimate(flops=flops, bytes_accessed=moved, transcendentals=0)


def swap_chip(x, count):
    return lax.ppermute(x, "space", [(i, i ^ 1) for i in range(count)])


def swap_across(x, count):
    pairs = [(i, i + 1) for i in range(1, count - 1, 2)]
    return lax.ppermute(x, "space", pairs + [(b, a) for a, b in pairs])


def phases_of(count):
    bits = [1 << k for k in range(count.bit_length() - 1)]
    out = [bits[:1]]
    for k in range(1, len(bits), 2):
        pair = bits[k : k + 2]
        out.append([pair[0]] if len(pair) == 1 else [pair[0], pair[1], pair[0] + pair[1]])
    return out


def local(flow, forcing, wet, depth, limiter, weights, bed, diffusivity):
    here, _, height, width = flow.shape
    tiles = width // LANES
    strips, groups = lax.axis_size("space"), lax.axis_size("cond")
    place = jnp.stack([lax.axis_index("cond") * here, lax.axis_index("space") % 2]).astype(jnp.int32)
    static = dict(depth=depth, limiter=limiter, bed=bed, diffusivity=diffusivity)
    reach = height + ABOVE + BELOW

    across, chip = [], []
    for which in range(here):
        names = MESSAGE[which]
        keys = ("flow", "forcing", "wet") + names[len(FLOW) :]
        arrays = dict(flow=flow, forcing=forcing, wet=wet, **static)
        size = offsets(names, tiles)[1]
        shape = jax.ShapeDtypeStruct((size, LANES), jnp.float32)
        out = pl.pallas_call(
            functools.partial(pack_kernel, names, keys),
            out_shape=(shape, shape),
            grid=(1,),
            in_specs=[SMEM] + [picked(arrays[k].shape, which) if k in ("flow", "forcing", "wet") else whole(arrays[k].shape) for k in keys],
            out_specs=(whole(shape.shape), whole(shape.shape)),
            compiler_params=pltpu.CompilerParams(**PARAMS),
            cost_estimate=cost(1000, 6 * height * width * 4 + size * LANES * 8),
            name=f"pack{which}",
        )(place, *(arrays[k] for k in keys))
        across.append(swap_across(out[0], strips))
        chip.append(swap_chip(out[1], strips))

    surface_shape = jax.ShapeDtypeStruct((here, height, width), jnp.float32)
    half_shape = jax.ShapeDtypeStruct((tiles // 2 * reach, LANES), jnp.float32)
    surface = low = high = None
    for which in range(here):
        arrays = dict(flow=flow, forcing=forcing, wet=wet, depth=depth, limiter=limiter)
        specs = {k: picked(v.shape, which) if k in ("flow", "forcing", "wet") else whole(v.shape) for k, v in arrays.items()}
        arrays.update(across=across[which], chip=chip[which], static_across=across[0], static_chip=chip[0])
        aliases = {}
        if which:
            arrays.update(low=low, high=high)
        for k in arrays:
            specs.setdefault(k, whole(arrays[k].shape))
        if which:
            arrays["surface"] = surface
            specs["surface"] = pl.BlockSpec(memory_space=pl.ANY)
            aliases = {2 + len(arrays) - 1: 0}
        keys = tuple(arrays)
        surface, low, high = pl.pallas_call(
            functools.partial(flow_kernel, which, keys),
            out_shape=(surface_shape, half_shape, half_shape),
            grid=(1,),
            in_specs=[SMEM, SMEM] + [specs[k] for k in keys],
            out_specs=(picked(surface_shape.shape, which), whole(half_shape.shape), whole(half_shape.shape)),
            scratch_shapes=[pltpu.VMEM((tiles + 2, 64, LANES), jnp.float32)] * 15,
            input_output_aliases=aliases,
            compiler_params=pltpu.CompilerParams(**PARAMS),
            cost_estimate=cost(2 * STEPS * 40 * 40 * width, 8 * height * width * 4),
            name=f"flow{which}",
        )(place, weights, *(arrays[k] for k in keys))

    bits = [1 << k for k in range(groups.bit_length() - 1)]
    for k, bit in enumerate(bits):
        low_other = lax.ppermute(low, "cond", [(i, i ^ bit) for i in range(groups)])
        flip = bits[-1 - k]
        high_other = lax.ppermute(high, "cond", [(i, i ^ flip) for i in range(groups)])
        if k + 1 < len(bits):
            low, high = low + low_other, high + high_other

    arrays = dict(low=low, low_other=low_other, high=high, high_other=high_other, bed=bed, diffusivity=diffusivity, across=across[1], chip=chip[1])
    block = jax.ShapeDtypeStruct((tiles, height, LANES), jnp.float32)
    small = jax.ShapeDtypeStruct((8, LANES), jnp.float32)
    rhs, image, moments = pl.pallas_call(
        functools.partial(moment_kernel, tuple(arrays)),
        out_shape=(block, block, small),
        grid=(1,),
        in_specs=[SMEM] + [whole(v.shape) for v in arrays.values()],
        out_specs=(whole(block.shape), whole(block.shape), whole(small.shape)),
        scratch_shapes=[pltpu.VMEM((tiles + 2, height + 24, LANES), jnp.float32)] * 5,
        compiler_params=pltpu.CompilerParams(**PARAMS),
        cost_estimate=cost(60 * height * width, 8 * height * width * 4),
        name="moments",
    )(place, *arrays.values())

    phases = phases_of(strips)
    for k, phase in enumerate(phases):
        others = [lax.ppermute(moments, "space", [(i, i ^ m) for i in range(strips)]) for m in phase]
        if k + 1 < len(phases):
            for other in others:
                moments = moments + other

    terms = [moments] + others
    bed_new = pl.pallas_call(
        final_kernel,
        out_shape=jax.ShapeDtypeStruct((height, width), jnp.float32),
        grid=(1,),
        in_specs=[whole(rhs.shape), whole(image.shape)] + [whole(small.shape)] * len(terms),
        out_specs=whole((height, width)),
        compiler_params=pltpu.CompilerParams(**PARAMS),
        cost_estimate=cost(3 * height * width, 3 * height * width * 4),
        name="final",
    )(rhs, image, *terms)
    return (surface, bed_new)


def solution(mesh):
    in_specs = (
        P("cond", None, "space", None),
        P("cond", None, "space", None),
        P("cond", "space", None),
        P("space", None),
        P("space", None),
        P(),
        P("space", None),
        P("space", None),
    )
    out_specs = (P("cond", "space", None), P("space", None))
    return jax.shard_map(local, mesh=mesh, in_specs=in_specs, out_specs=out_specs, check_vma=False)
```

time: 206 us -> 73.5 us (0.36)
  starting transfers between devices: 72.4 us -> 22.9 us
  waiting for transfers between devices: 56.7 us -> 9.07 us
  Pallas kernels: 0 us -> 35.5 us
  blocking collectives: 30.5 us -> 0 us
  between operations: 20.6 us -> 0.74 us
  other arithmetic: 19.7 us -> 0.1 us
    ppermute x30 -> x12, starting transfers between devices: 72.4 us -> 22.9 us  [the longest x4 7.91 us: local(): lax.ppermute(moments, 'space', [(i, i ^ m) for i in range(strips)])]
    psum x1 -> x0, waiting for transfers between devices: 40.1 us -> none  [local(): portion = lax.psum(own_part, 'cond')]
    pallas_call x0 -> x6, Pallas kernels: none -> 35.5 us  [the longest x2 29.5 us: local(): pl.pallas_call(functools.partial(flow_kernel, which, keys), out_shape=(su...]
    psum x2 -> x0, blocking collectives: 30.5 us -> none  [reduce_all(): return lax.psum(values, 'space')]
    ppermute x30 -> x12, waiting for transfers between devices: 16.6 us -> 9.07 us  [the longest x4 4.76 us: local(): lax.ppermute(moments, 'space', [(i, i ^ m) for i in range(strips)])]
    another operation x15 -> x1, other arithmetic: 5.53 us -> 0.08 us  [local(): jnp.stack([lax.axis_index('cond') * here, lax.axis_index('space') % 2])]
    add x6 -> x3, other arithmetic: 3.34 us -> 0.03 us  [the longest x2 0.02 us: local(): low, high = (low + low_other, high + high_other)]
    mul x8 -> x0, other arithmetic: 3.1 us -> none  [the longest x4 2.26 us: second_section(): 0.5 * (state_now + first_section + time_step * tendency(first_section, ri...]
  transfers between devices with their start and end apart: 31 -> 12, of which waited for: 9 -> 6; matrix products, arithmetic and copies ran while one was open for 3% -> 0% of each run, Pallas kernels for 0% -> 21%
where the time goes in v1:
time: 73.5 us; the launch traced here: 73.2 us
  Pallas kernels  35.5 us (48%)
  starting transfers between devices  22.9 us (31%)
  waiting for transfers between devices  9.07 us (12%)
  local copies, waits for them, and re-layouts  4.96 us (7%)
  between operations  0.74 us (1%)
    pallas_call x2, Pallas kernels, local(): pl.pallas_call(functools.partial(flow_kernel, which, keys), out_shape=(su...  29.5 us
    ppermute x4, starting transfers between devices, local(): lax.ppermute(moments, 'space', [(i, i ^ m) for i in range(strips)])  7.91 us
    ppermute x2, starting transfers between devices, swap_chip(): return lax.ppermute(x, 'space', [(i, i ^ 1) for i in range(count)])  7.41 us
    unnamed x20, local copies, waits for them, and re-layouts  4.96 us
    ppermute x4, waiting for transfers between devices, local(): lax.ppermute(moments, 'space', [(i, i ^ m) for i in range(strips)])  4.76 us
    pallas_call x1, Pallas kernels, local(): pl.pallas_call(functools.partial(moment_kernel, tuple(arrays)), out_shape...  3.47 us
    ppermute x2, starting transfers between devices, local(): lax.ppermute(high, 'cond', [(i, i ^ flip) for i in range(groups)])  3.08 us
    ppermute x2, starting transfers between devices, local(): low_other = lax.ppermute(low, 'cond', [(i, i ^ bit) for i in range(groups)])  3.08 us
  transfers between devices with their start and end apart: 12, of which 6 were waited for; matrix products, arithmetic and copies ran while one was open for 0% of the time, Pallas kernels for 21%

profile of v1, /device:TPU:0, one launch (start us, length us, event | category | flops | bytes accessed | tf_op | source)
XLA Modules:
  0.0 73.2 jit_solution(4237093981680395306)
XLA Ops:
  0.6 0.1 pad_add_fusion.place_ref
  0.7 0.0 copy-start
  0.7 1.1 %copy-done = f32[2,3,16,2048]{3,2,1,0:T(8,128)S(1)} copy-done((f32[2,3,16,2048]{3,2,1,0:T(8,128)S(1)}, f32[2,3,16,2048]{3,2,1,0:T(8,128)}, u32[]{:S(2)}) %copy-start) | copy-done | bytes 786456
  1.9 0.0 copy-start.1
  1.9 1.0 %copy-done.1 = f32[2,2,16,2048]{3,2,1,0:T(8,128)S(1)} copy-done((f32[2,2,16,2048]{3,2,1,0:T(8,128)S(1)}, f32[2,2,16,2048]{3,2,1,0:T(8,128)}, u32[]{:S(2)}) %copy-start.1) | copy-done | bytes 524312
  2.9 0.0 copy-start.2
  2.9 0.9 %copy-done.2 = s32[2,16,2048]{2,1,0:T(8,128)S(1)} copy-done((s32[2,16,2048]{2,1,0:T(8,128)S(1)}, s32[2,16,2048]{2,1,0:T(8,128)}, u32[]{:S(2)}) %copy-start.2) | copy-done | bytes 262168
  3.8 0.0 copy-start.3
  3.8 0.9 %copy-done.3 = f32[16,2048]{1,0:T(8,128)S(1)} copy-done((f32[16,2048]{1,0:T(8,128)S(1)}, f32[16,2048]{1,0:T(8,128)}, u32[]{:S(2)}) %copy-start.3) | copy-done | bytes 131096
  4.7 0.0 copy-start.5
  4.7 0.9 %copy-done.5 = s32[16,2048]{1,0:T(8,128)S(1)} copy-done((s32[16,2048]{1,0:T(8,128)S(1)}, s32[16,2048]{1,0:T(8,128)}, u32[]{:S(2)}) %copy-start.5) | copy-done | bytes 131096
  5.7 0.0 copy-start.7
  5.7 0.0 copy-start.8
  5.7 0.8 %pack0.1 = (f32[1216,128]{1,0:T(8,128)S(1)}, f32[1216,128]{1,0:T(8,128)S(1)}) custom-call(s32[2]{0:T(128)S(1)} %pad_add_fusion.place_ref, f32[2,3,16,2048]{3,2,1,0:T(8,128)S(1)} %copy-done, f32[2,2,16,2048]{3,2,1,0:T(8,128)S(1)} %copy-done.1, s32[2,16,2048]{2,1,0:T(8,128)S(1)} %copy-done.2, f32[16,2048]{1,0:T(8,128)S(1)} %copy-done.3, s32[16,2048]{1,0:T(8,128)S(1)} %copy-done.5), custom_call_target="tpu_custom_call" | custom-call | flops 1000 | bytes 2031616 | tf_op jit(solution)/shard_map/pack0/pallas_call | solution.py:409
  6.5 0.7 collective-permute-start.2
  7.2 0.0 copy-start.4
  7.2 0.0 copy-start.6
  7.2 4.4 %collective-permute-start.3 = (f32[1216,128]{1,0:T(8,128)S(1)}, f32[1216,128]{1,0:T(8,128)S(1)}, u32[]{:S(2)}, u32[]{:S(2)}) collective-permute-start(f32[1216,128]{1,0:T(8,128)S(1)} %get-tuple-element.18), channel_id=1, source_target_pairs={{0,1},{1,0},{2,3},{3,2},{4,5},{5,4},{6,7},{7,6},{8,9},{9,8},{10,11... | collective-permute-start | bytes 1867784 | tf_op jit(solution)/shard_map/ppermute | solution.py:377
  11.6 0.0 copy-done.7
  11.6 0.0 copy-done.8
  11.6 0.8 %pack1.1 = (f32[1056,128]{1,0:T(8,128)S(1)}, f32[1056,128]{1,0:T(8,128)S(1)}) custom-call(s32[2]{0:T(128)S(1)} %pad_add_fusion.place_ref, f32[2,3,16,2048]{3,2,1,0:T(8,128)S(1)} %copy-done, f32[2,2,16,2048]{3,2,1,0:T(8,128)S(1)} %copy-done.1, s32[2,16,2048]{2,1,0:T(8,128)S(1)} %copy-done.2, f32[16,2048]{1,0:T(8,128)S(1)} %copy-done.7, f32[16,2048]{1,0:T(8,128)S(1)} %copy-done.8), custom_call_target="tpu_custom_call" | custom-call | flops 1000 | bytes 1867776 | tf_op jit(solution)/shard_map/pack1/pallas_call | solution.py:409
  12.4 0.0 copy-start.9
  12.5 0.7 collective-permute-start
  13.2 3.0 %collective-permute-start.1 = (f32[1056,128]{1,0:T(8,128)S(1)}, f32[1056,128]{1,0:T(8,128)S(1)}, u32[]{:S(2)}, u32[]{:S(2)}) collective-permute-start(f32[1056,128]{1,0:T(8,128)S(1)} %get-tuple-element.16), channel_id=1, source_target_pairs={{0,1},{1,0},{2,3},{3,2},{4,5},{5,4},{6,7},{7,6},{8,9},{9,8},{10,11... | collective-permute-start | bytes 1622024 | tf_op jit(solution)/shard_map/ppermute | solution.py:377
  16.1 0.0 collective-permute-done.2.args_5_.args_7_
  16.1 0.0 collective-permute-done.3.args_6_.args_8_
  16.1 0.0 copy-done.4
  16.1 0.0 copy-done.6
  16.1 0.0 copy-done.9
  16.2 14.8 %flow0.1 = (f32[2,16,2048]{2,1,0:T(8,128)}, f32[152,128]{1,0:T(8,128)S(1)}, f32[152,128]{1,0:T(8,128)S(1)}) custom-call(s32[2]{0:T(128)S(1)} %pad_add_fusion.place_ref, s32[8]{0:T(128)S(1)} %copy-done.9, f32[2,3,16,2048]{3,2,1,0:T(8,128)S(1)} %copy-done, f32[2,2,16,2048]{3,2,1,0:T(8,128)S(1)} %copy-done.1, s32[2,16,2048]{2,1,0:T(8,128)S(1)} %copy-done.2, ...), custom_call_target="tpu_custom_call" | custom-call | flops 26214400 | bytes 1048576 | tf_op jit(solution)/shard_map/flow0/pallas_call | solution.py:439
  30.9 0.0 collective-permute-done.args_5_.args_6_
  30.9 0.0 collective-permute-done.1.args_6_.args_7_
  30.9 14.8 %flow1.1 = (f32[2,16,2048]{2,1,0:T(8,128)}, f32[152,128]{1,0:T(8,128)S(1)}, f32[152,128]{1,0:T(8,128)S(1)}) custom-call(s32[2]{0:T(128)S(1)} %pad_add_fusion.place_ref, s32[8]{0:T(128)S(1)} %copy-done.9, f32[2,3,16,2048]{3,2,1,0:T(8,128)S(1)} %copy-done, f32[2,2,16,2048]{3,2,1,0:T(8,128)S(1)} %copy-done.1, ...), custom_call_target="tpu_custom_call", output_to_operand_aliasing={{0}: (13, {})} | custom-call | flops 26214400 | bytes 1048576 | tf_op jit(solution)/shard_map/flow1/pallas_call | solution.py:439
  45.7 1.5 %collective-permute-start.4 = (f32[152,128]{1,0:T(8,128)S(1)}, f32[152,128]{1,0:T(8,128)S(1)}, u32[]{:S(2)}, u32[]{:S(2)}) collective-permute-start(f32[152,128]{1,0:T(8,128)S(1)} %get-tuple-element.23), channel_id=1, source_target_pairs={{0,8},{8,0},{16,24},{24,16},{1,9},{9,1},{17,25},{25,17},{2,10},{10... | collective-permute-start | bytes 233480 | tf_op jit(solution)/shard_map/ppermute | solution.py:454
  47.2 1.5 %collective-permute-start.6 = (f32[152,128]{1,0:T(8,128)S(1)}, f32[152,128]{1,0:T(8,128)S(1)}, u32[]{:S(2)}, u32[]{:S(2)}) collective-permute-start(f32[152,128]{1,0:T(8,128)S(1)} %get-tuple-element.24), channel_id=1, source_target_pairs={{0,16},{8,24},{16,0},{24,8},{1,17},{9,25},{17,1},{25,9},{2,18},{10... | collective-permute-start | bytes 233480 | tf_op jit(solution)/shard_map/ppermute | solution.py:456
  48.7 1.4 %collective-permute-done.4 = f32[152,128]{1,0:T(8,128)S(1)} collective-permute-done((f32[152,128]{1,0:T(8,128)S(1)}, f32[152,128]{1,0:T(8,128)S(1)}, u32[]{:S(2)}, u32[]{:S(2)}) %collective-permute-start.4) | collective-permute-done | bytes 77856 | tf_op jit(solution)/shard_map/ppermute | solution.py:454
  50.1 1.6 %collective-permute-start.5 = (f32[152,128]{1,0:T(8,128)S(1)}, f32[152,128]{1,0:T(8,128)S(1)}, u32[]{:S(2)}, u32[]{:S(2)}) collective-permute-start(f32[152,128]{1,0:T(8,128)S(1)} %add.14.args_0_), channel_id=1, source_target_pairs={{0,16},{8,24},{16,0},{24,8},{1,17},{9,25},{17,1},{25,9},{2,18},{10... | collective-permute-start | bytes 233480 | tf_op jit(solution)/shard_map/ppermute | solution.py:454
  51.7 0.0 collective-permute-done.6
  51.7 1.6 %collective-permute-start.7 = (f32[152,128]{1,0:T(8,128)S(1)}, f32[152,128]{1,0:T(8,128)S(1)}, u32[]{:S(2)}, u32[]{:S(2)}) collective-permute-start(f32[152,128]{1,0:T(8,128)S(1)} %add.15.args_2_), channel_id=1, source_target_pairs={{0,8},{8,0},{16,24},{24,16},{1,9},{9,1},{17,25},{25,17},{2,10},{10... | collective-permute-start | bytes 233480 | tf_op jit(solution)/shard_map/ppermute | solution.py:456
  53.3 1.3 %collective-permute-done.5.args_1_ = f32[152,128]{1,0:T(8,128)S(1)} collective-permute-done((f32[152,128]{1,0:T(8,128)S(1)}, f32[152,128]{1,0:T(8,128)S(1)}, u32[]{:S(2)}, u32[]{:S(2)}) %collective-permute-start.5) | collective-permute-done | bytes 77856 | tf_op jit(solution)/shard_map/ppermute | solution.py:454
  54.6 1.6 %collective-permute-done.7.args_3_ = f32[152,128]{1,0:T(8,128)S(1)} collective-permute-done((f32[152,128]{1,0:T(8,128)S(1)}, f32[152,128]{1,0:T(8,128)S(1)}, u32[]{:S(2)}, u32[]{:S(2)}) %collective-permute-start.7) | collective-permute-done | bytes 77856 | tf_op jit(solution)/shard_map/ppermute | solution.py:456
  56.2 3.5 %moments.1 = (f32[16,16,128]{2,1,0:T(8,128)S(1)}, f32[16,16,128]{2,1,0:T(8,128)S(1)}, f32[8,128]{1,0:T(8,128)S(1)}) custom-call(s32[2]{0:T(128)S(1)} %pad_add_fusion.place_ref, f32[152,128]{1,0:T(8,128)S(1)} %add.14.args_0_, f32[152,128]{1,0:T(8,128)S(1)} %collective-permute-done.5.args_1_, f32[152,128]{1,0:T(8,128)S(1)} %add.15.args_2_, ...), custom_call_target="tpu_custom_call" | custom-call | flops 1966080 | bytes 1048576 | tf_op jit(solution)/shard_map/moments/pallas_call | solution.py:463
  59.6 0.8 %collective-permute-start.8 = (f32[8,128]{1,0:T(8,128)S(1)}, f32[8,128]{1,0:T(8,128)S(1)}, u32[]{:S(2)}, u32[]{:S(2)}) collective-permute-start(f32[8,128]{1,0:T(8,128)S(1)} %get-tuple-element.27), channel_id=1, source_target_pairs={{0,1},{1,0},{2,3},{3,2},{4,5},{5,4},{6,7},{7,6},{8,9},{9,8},{10,11... | collective-permute-start | bytes 12296 | tf_op jit(solution)/shard_map/ppermute | solution.py:477
  60.4 0.8 %collective-permute-done.8 = f32[8,128]{1,0:T(8,128)S(1)} collective-permute-done((f32[8,128]{1,0:T(8,128)S(1)}, f32[8,128]{1,0:T(8,128)S(1)}, u32[]{:S(2)}, u32[]{:S(2)}) %collective-permute-start.8) | collective-permute-done | bytes 4128 | tf_op jit(solution)/shard_map/ppermute | solution.py:477
  61.2 6.6 %collective-permute-start.11 = (f32[8,128]{1,0:T(8,128)S(1)}, f32[8,128]{1,0:T(8,128)S(1)}, u32[]{:S(2)}, u32[]{:S(2)}) collective-permute-start(f32[8,128]{1,0:T(8,128)S(1)} %add.16.args_0_), channel_id=1, source_target_pairs={{0,6},{1,7},{2,4},{3,5},{4,2},{5,3},{6,0},{7,1},{8,14},{9,15},{10,... | collective-permute-start | bytes 12296 | tf_op jit(solution)/shard_map/ppermute | solution.py:477
  67.8 0.0 collective-permute-start.10
  67.8 0.6 collective-permute-start.9
  68.4 1.0 %collective-permute-done.11.args_3_ = f32[8,128]{1,0:T(8,128)S(1)} collective-permute-done((f32[8,128]{1,0:T(8,128)S(1)}, f32[8,128]{1,0:T(8,128)S(1)}, u32[]{:S(2)}, u32[]{:S(2)}) %collective-permute-start.11) | collective-permute-done | bytes 4128 | tf_op jit(solution)/shard_map/ppermute | solution.py:477
  69.4 2.9 %collective-permute-done.10.args_2_ = f32[8,128]{1,0:T(8,128)S(1)} collective-permute-done((f32[8,128]{1,0:T(8,128)S(1)}, f32[8,128]{1,0:T(8,128)S(1)}, u32[]{:S(2)}, u32[]{:S(2)}) %collective-permute-start.10) | collective-permute-done | bytes 4128 | tf_op jit(solution)/shard_map/ppermute | solution.py:477
  72.3 0.0 collective-permute-done.9.args_1_
  72.3 0.9 %final.1 = f32[16,2048]{1,0:T(8,128)} custom-call(f32[16,16,128]{2,1,0:T(8,128)S(1)} %get-tuple-element.25.rhs_ref, f32[16,16,128]{2,1,0:T(8,128)S(1)} %get-tuple-element.26.image_ref, f32[8,128]{1,0:T(8,128)S(1)} %add.16.args_0_, f32[8,128]{1,0:T(8,128)S(1)} %collective-permute-done.9.args_1_, f32[8,128]{1,0:T(8,128)S(1)} %collective-permute-done.10.args_2_, ...), custom_call_target="tpu_custom_call" | custom-call | flops 98304 | bytes 393216 | tf_op jit(solution)/shard_map/final/pallas_call | solution.py:483
  (3 shorter events, 0.0 us)
Async XLA Ops:
  0.7 1.1 %copy-start = (f32[2,3,16,2048]{3,2,1,0:T(8,128)S(1)}, f32[2,3,16,2048]{3,2,1,0:T(8,128)}, u32[]{:S(2)}) copy-start(f32[2,3,16,2048]{3,2,1,0:T(8,128)} %args_0_.10) | copy-start | bytes 2359300
  1.9 1.0 %copy-start.1 = (f32[2,2,16,2048]{3,2,1,0:T(8,128)S(1)}, f32[2,2,16,2048]{3,2,1,0:T(8,128)}, u32[]{:S(2)}) copy-start(f32[2,2,16,2048]{3,2,1,0:T(8,128)} %args_1_.10) | copy-start | bytes 1572868
  2.9 0.9 %copy-start.2 = (s32[2,16,2048]{2,1,0:T(8,128)S(1)}, s32[2,16,2048]{2,1,0:T(8,128)}, u32[]{:S(2)}) copy-start(s32[2,16,2048]{2,1,0:T(8,128)} %args_2_.10) | copy-start | bytes 786436
  3.8 0.9 %copy-start.3 = (f32[16,2048]{1,0:T(8,128)S(1)}, f32[16,2048]{1,0:T(8,128)}, u32[]{:S(2)}) copy-start(f32[16,2048]{1,0:T(8,128)} %args_3_.10) | copy-start | bytes 393220
  4.7 0.9 %copy-start.5 = (s32[16,2048]{1,0:T(8,128)S(1)}, s32[16,2048]{1,0:T(8,128)}, u32[]{:S(2)}) copy-start(s32[16,2048]{1,0:T(8,128)} %args_4_.11) | copy-start | bytes 393220
  5.7 6.0 %copy-start.7 = (f32[16,2048]{1,0:T(8,128)S(1)}, f32[16,2048]{1,0:T(8,128)}, u32[]{:S(2)}) copy-start(f32[16,2048]{1,0:T(8,128)} %args_4_.12) | copy-start | bytes 393220
  5.7 6.0 %copy-start.8 = (f32[16,2048]{1,0:T(8,128)S(1)}, f32[16,2048]{1,0:T(8,128)}, u32[]{:S(2)}) copy-start(f32[16,2048]{1,0:T(8,128)} %args_5_.4) | copy-start | bytes 393220
  6.5 9.7 %collective-permute-start.2 = (f32[1216,128]{1,0:T(8,128)S(1)}, f32[1216,128]{1,0:T(8,128)S(1)}, u32[]{:S(2)}, u32[]{:S(2)}) collective-permute-start(f32[1216,128]{1,0:T(8,128)S(1)} %get-tuple-element.17), channel_id=1, source_target_pairs={{1,2},{3,4},{5,6},{2,1},{4,3},{6,5},{9,10},{11,12},{13,14},{10,9},... | collective-permute-start | bytes 1867784 | tf_op jit(solution)/shard_map/ppermute | solution.py:382
  7.2 9.0 %copy-start.4 = (f32[16,2048]{1,0:T(8,128)S(1)}, f32[16,2048]{1,0:T(8,128)}, u32[]{:S(2)}) copy-start(f32[16,2048]{1,0:T(8,128)} %args_3_.10) | copy-start | bytes 393220
  7.2 9.0 %copy-start.6 = (s32[16,2048]{1,0:T(8,128)S(1)}, s32[16,2048]{1,0:T(8,128)}, u32[]{:S(2)}) copy-start(s32[16,2048]{1,0:T(8,128)} %args_4_.11) | copy-start | bytes 393220
  7.2 8.9 %collective-permute-start.3 = (f32[1216,128]{1,0:T(8,128)S(1)}, f32[1216,128]{1,0:T(8,128)S(1)}, u32[]{:S(2)}, u32[]{:S(2)}) collective-permute-start(f32[1216,128]{1,0:T(8,128)S(1)} %get-tuple-element.18), channel_id=1, source_target_pairs={{0,1},{1,0},{2,3},{3,2},{4,5},{5,4},{6,7},{7,6},{8,9},{9,8},{10,11... | collective-permute-start | bytes 1867784 | tf_op jit(solution)/shard_map/ppermute | solution.py:377
  12.4 3.7 %copy-start.9 = (s32[8]{0:T(128)S(1)}, s32[8]{0:T(128)}, u32[]{:S(2)}) copy-start(s32[8]{0:T(128)} %weights_ref.3) | copy-start | bytes 100
  12.5 18.5 %collective-permute-start = (f32[1056,128]{1,0:T(8,128)S(1)}, f32[1056,128]{1,0:T(8,128)S(1)}, u32[]{:S(2)}, u32[]{:S(2)}) collective-permute-start(f32[1056,128]{1,0:T(8,128)S(1)} %get-tuple-element.15), channel_id=1, source_target_pairs={{1,2},{3,4},{5,6},{2,1},{4,3},{6,5},{9,10},{11,12},{13,14},{10,9},... | collective-permute-start | bytes 1622024 | tf_op jit(solution)/shard_map/ppermute | solution.py:382
  13.2 17.8 %collective-permute-start.1 = (f32[1056,128]{1,0:T(8,128)S(1)}, f32[1056,128]{1,0:T(8,128)S(1)}, u32[]{:S(2)}, u32[]{:S(2)}) collective-permute-start(f32[1056,128]{1,0:T(8,128)S(1)} %get-tuple-element.16), channel_id=1, source_target_pairs={{0,1},{1,0},{2,3},{3,2},{4,5},{5,4},{6,7},{7,6},{8,9},{9,8},{10,11... | collective-permute-start | bytes 1622024 | tf_op jit(solution)/shard_map/ppermute | solution.py:377
  45.7 4.4 %collective-permute-start.4 = (f32[152,128]{1,0:T(8,128)S(1)}, f32[152,128]{1,0:T(8,128)S(1)}, u32[]{:S(2)}, u32[]{:S(2)}) collective-permute-start(f32[152,128]{1,0:T(8,128)S(1)} %get-tuple-element.23), channel_id=1, source_target_pairs={{0,8},{8,0},{16,24},{24,16},{1,9},{9,1},{17,25},{25,17},{2,10},{10... | collective-permute-start | bytes 233480 | tf_op jit(solution)/shard_map/ppermute | solution.py:454
  47.2 4.5 %collective-permute-start.6 = (f32[152,128]{1,0:T(8,128)S(1)}, f32[152,128]{1,0:T(8,128)S(1)}, u32[]{:S(2)}, u32[]{:S(2)}) collective-permute-start(f32[152,128]{1,0:T(8,128)S(1)} %get-tuple-element.24), channel_id=1, source_target_pairs={{0,16},{8,24},{16,0},{24,8},{1,17},{9,25},{17,1},{25,9},{2,18},{10... | collective-permute-start | bytes 233480 | tf_op jit(solution)/shard_map/ppermute | solution.py:456
  50.1 4.5 %collective-permute-start.5 = (f32[152,128]{1,0:T(8,128)S(1)}, f32[152,128]{1,0:T(8,128)S(1)}, u32[]{:S(2)}, u32[]{:S(2)}) collective-permute-start(f32[152,128]{1,0:T(8,128)S(1)} %add.14.args_0_), channel_id=1, source_target_pairs={{0,16},{8,24},{16,0},{24,8},{1,17},{9,25},{17,1},{25,9},{2,18},{10... | collective-permute-start | bytes 233480 | tf_op jit(solution)/shard_map/ppermute | solution.py:454
  51.7 4.5 %collective-permute-start.7 = (f32[152,128]{1,0:T(8,128)S(1)}, f32[152,128]{1,0:T(8,128)S(1)}, u32[]{:S(2)}, u32[]{:S(2)}) collective-permute-start(f32[152,128]{1,0:T(8,128)S(1)} %add.15.args_2_), channel_id=1, source_target_pairs={{0,8},{8,0},{16,24},{24,16},{1,9},{9,1},{17,25},{25,17},{2,10},{10... | collective-permute-start | bytes 233480 | tf_op jit(solution)/shard_map/ppermute | solution.py:456
  59.6 1.6 %collective-permute-start.8 = (f32[8,128]{1,0:T(8,128)S(1)}, f32[8,128]{1,0:T(8,128)S(1)}, u32[]{:S(2)}, u32[]{:S(2)}) collective-permute-start(f32[8,128]{1,0:T(8,128)S(1)} %get-tuple-element.27), channel_id=1, source_target_pairs={{0,1},{1,0},{2,3},{3,2},{4,5},{5,4},{6,7},{7,6},{8,9},{9,8},{10,11... | collective-permute-start | bytes 12296 | tf_op jit(solution)/shard_map/ppermute | solution.py:477
  61.2 8.2 %collective-permute-start.11 = (f32[8,128]{1,0:T(8,128)S(1)}, f32[8,128]{1,0:T(8,128)S(1)}, u32[]{:S(2)}, u32[]{:S(2)}) collective-permute-start(f32[8,128]{1,0:T(8,128)S(1)} %add.16.args_0_), channel_id=1, source_target_pairs={{0,6},{1,7},{2,4},{3,5},{4,2},{5,3},{6,0},{7,1},{8,14},{9,15},{10,... | collective-permute-start | bytes 12296 | tf_op jit(solution)/shard_map/ppermute | solution.py:477
  67.8 4.5 %collective-permute-start.10 = (f32[8,128]{1,0:T(8,128)S(1)}, f32[8,128]{1,0:T(8,128)S(1)}, u32[]{:S(2)}, u32[]{:S(2)}) collective-permute-start(f32[8,128]{1,0:T(8,128)S(1)} %add.16.args_0_), channel_id=1, source_target_pairs={{0,4},{1,5},{2,6},{3,7},{4,0},{5,1},{6,2},{7,3},{8,12},{9,13},{10,... | collective-permute-start | bytes 12296 | tf_op jit(solution)/shard_map/ppermute | solution.py:477
  67.8 4.5 %collective-permute-start.9 = (f32[8,128]{1,0:T(8,128)S(1)}, f32[8,128]{1,0:T(8,128)S(1)}, u32[]{:S(2)}, u32[]{:S(2)}) collective-permute-start(f32[8,128]{1,0:T(8,128)S(1)} %add.16.args_0_), channel_id=1, source_target_pairs={{0,2},{1,3},{2,0},{3,1},{4,6},{5,7},{6,4},{7,5},{8,10},{9,11},{10,... | collective-permute-start | bytes 12296 | tf_op jit(solution)/shard_map/ppermute | solution.py:477

commit v2 on v1

v2 whole, which is shorter than its diff:
```python
import functools

import jax
import jax.numpy as jnp
from jax import lax
from jax.experimental import pallas as pl
from jax.experimental.pallas import tpu as pltpu
from jax.sharding import PartitionSpec as P

STEPS = 4

time_step = 0.4
gravity = 1.0
friction = 0.1
transport_base = 0.5
morph_factor = 1.0
slope_coeff = 1.0

LANES = 128
(
    ELEV, FIRST, SECOND, FORCE_A, FORCE_B, HALF, KEEP, WET_DEPTH, KEEP_AHEAD, WET_AHEAD, INVERSE, LIMITER,
    ELEV_MID, FIRST_MID, SECOND_MID, DEPTH, FLUX_A, FLUX_B, BED, DIFFUSIVITY, FLOW_IN, FORCING, WET,
    ACROSS, CHIP, STATIC_ACROSS, STATIC_CHIP, LOW, HIGH, LOW_OTHER, HIGH_OTHER, SURFACE, BASE, DERIVED,
) = range(34)

ABOVE, BELOW = 1, 2
OWN = 24
UNROLL = 16


def rows_needed(height):
    flux = (-ABOVE - 1, height + BELOW)
    need = [{ELEV: (0, height - 1), FIRST: flux, SECOND: flux}]
    for _ in range(2 * STEPS):
        e, f, s = need[0][ELEV], need[0][FIRST], need[0][SECOND]
        need.insert(0, {ELEV: (min(e[0], f[0] - 1, s[0]), max(e[1], f[1] + 1, s[1])), FIRST: (min(f[0], e[0] - 1), max(f[1], e[1] + 1)), SECOND: (min(s[0], e[0]), max(s[1], e[1]))})
    return need


def halo_rows(height):
    need = rows_needed(height)
    past = lambda stage, name: need[stage][name][1] - (height - 1)
    return {ELEV: past(0, ELEV), FIRST: past(0, FIRST), SECOND: past(0, SECOND), FORCE_A: past(1, FIRST), FORCE_B: past(1, SECOND), HALF: past(1, ELEV), DEPTH: past(1, FIRST), LIMITER: BELOW + 1, BED: BELOW, DIFFUSIVITY: BELOW}


AHEAD = (SECOND, FORCE_B, KEEP_AHEAD, WET_AHEAD)
FLOW = (ELEV, FIRST, SECOND, FORCE_A, FORCE_B, HALF)
BASE_NAMES = FLOW + (DEPTH, LIMITER)
DERIVED_NAMES = (KEEP, WET_DEPTH, KEEP_AHEAD, WET_AHEAD, INVERSE)
SPAN = 64


def message(which, last):
    names = FLOW
    if which == 0:
        names = names + (DEPTH, LIMITER)
    if which == last:
        names = names + (BED, DIFFUSIVITY)
    return names


def offsets(names, tiles, height):
    places, at, count = {}, 0, halo_rows(height)
    for name in names:
        places[name] = at
        at += (tiles + (name in AHEAD)) * count[name]
    return places, -(-at // 8) * 8


def lanes_of(tile):
    return pl.ds(pl.multiple_of(tile * LANES, LANES), LANES)


def lane_index():
    return lax.broadcasted_iota(jnp.int32, (8, LANES), 1)


def ahead(here, after):
    return pltpu.roll(jnp.where(lane_index() == 0, after, here), LANES - 1, 1)


def behind(here, before):
    return pltpu.roll(jnp.where(lane_index() == LANES - 1, before, here), 1, 1)


def prepare_kernel(which, last, keys, place_ref, *args):
    n = len(keys)
    hbm = dict(zip(keys, args[:n]))
    args = args[n + bool(which) :]
    across_ref, chip_ref, base_ref = args[:3]
    args = args[3:]
    if which:
        derived_ref, args = args[0], args[1:]
    held = dict(zip(keys, args[:n]))
    second_ref, force_ref, sem = args[n:]
    copies = []
    for slot, key in enumerate(keys):
        source = hbm[key].at[which] if key in (FLOW_IN, FORCING, WET) else hbm[key]
        copies.append(pltpu.make_async_copy(source, held[key], sem.at[slot]))
        copies[-1].start()
    height, tiles = held[DEPTH].shape[0], held[DEPTH].shape[1] // LANES
    names = message(which, last)
    places, _ = offsets(names, tiles, height)
    count = halo_rows(height)
    slot_of = {name: k for k, name in enumerate(BASE_NAMES)}

    zero = jnp.zeros((height, LANES), jnp.float32)
    for ref in (second_ref, force_ref):
        for edge in (0, tiles + 1):
            ref[edge, :, :] = zero
    zero = jnp.zeros((SPAN, LANES), jnp.float32)
    for name in (ELEV, HALF, DEPTH):
        for edge in (0, tiles + 1):
            base_ref[slot_of[name], edge, :, :] = zero
    for copy in copies:
        copy.wait()

    def derive(tile, carry):
        at = tile + 1
        for row in range(0, height, 8):
            rows = slice(row, row + 8)

            def put(name, value):
                base_ref[slot_of[name], at, OWN + row : OWN + row + 8, :] = value

            depth = held[DEPTH][rows, lanes_of(tile)]
            half = (0.5 * time_step) * held[WET][rows, lanes_of(tile)].astype(jnp.float32)
            push = 2.0 * half * depth
            put(ELEV, held[FLOW_IN][0, rows, lanes_of(tile)])
            put(FIRST, depth * held[FLOW_IN][1, rows, lanes_of(tile)])
            put(FORCE_A, push * held[FORCING][0, rows, lanes_of(tile)])
            put(HALF, half)
            put(DEPTH, depth)
            put(LIMITER, held[LIMITER][rows, lanes_of(tile)].astype(jnp.float32))
            second_ref[at, rows, :] = depth * held[FLOW_IN][2, rows, lanes_of(tile)]
            force_ref[at, rows, :] = push * held[FORCING][1, rows, lanes_of(tile)]
        return carry

    lax.fori_loop(0, tiles, derive, 0, unroll=2)

    def shift(block, carry):
        for row in range(0, height, 8):
            rows = slice(row, row + 8)
            for name, ref in ((SECOND, second_ref), (FORCE_B, force_ref)):
                moved = ahead(ref[block, rows, :], ref[block + 1, rows, :])
                base_ref[slot_of[name], block, OWN + row : OWN + row + 8, :] = moved
        return carry

    shift(0, 0)
    lax.fori_loop(1, tiles + 1, shift, 0, unroll=4)

    def fill(head_ref, tail_ref):
        def give(name, block, chunk):
            rows = count[name]
            where = pl.ds(places[name] + chunk * rows, rows)
            if name in slot_of:
                head_ref[where, :] = base_ref[slot_of[name], block, OWN : OWN + rows, :]
                tail_ref[where, :] = base_ref[slot_of[name], block, OWN + height - rows : OWN + height, :]
            else:
                head_ref[where, :] = held[name][:rows, lanes_of(chunk)]
                tail_ref[where, :] = held[name][height - rows :, lanes_of(chunk)]

        def body(tile, carry):
            for name in names:
                give(name, tile + 1, tile + (name in AHEAD))
            return carry

        for name in names:
            if name in AHEAD:
                give(name, 0, 0)
        lax.fori_loop(0, tiles, body, 0, unroll=2)

    odd = place_ref[1]

    @pl.when(odd == 0)
    def _():
        fill(across_ref, chip_ref)

    @pl.when(odd == 1)
    def _():
        fill(chip_ref, across_ref)

    if which:
        derive_kernel(base_ref, derived_ref, height=height)


def derive_rows(base, derived, block, row, names):
    rows = slice(row, row + 8)

    def put(name, value):
        derived[DERIVED_NAMES.index(name), block, rows, :] = value

    half_at, depth_at = BASE_NAMES.index(HALF), BASE_NAMES.index(DEPTH)
    half, depth = base[half_at, block, rows, :], base[depth_at, block, rows, :]
    if KEEP in names:
        put(KEEP, 1.0 - (2.0 * friction) * half)
        put(WET_DEPTH, gravity * half * depth)
    if INVERSE in names:
        put(INVERSE, jnp.where(depth > 0.0, 1.0 / depth, 0.0))
    if KEEP_AHEAD in names:
        half = ahead(half, base[half_at, block + 1, rows, :])
        depth = ahead(depth, base[depth_at, block + 1, rows, :])
        put(KEEP_AHEAD, 1.0 - (2.0 * friction) * half)
        put(WET_AHEAD, gravity * half * depth)


def derive_kernel(base_ref, derived_ref, *, height):
    tiles = base_ref.shape[1] - 2

    def body(block, carry):
        for row in range(OWN, OWN + height, 8):
            derive_rows(base_ref, derived_ref, block, row, DERIVED_NAMES)
        return carry

    body(0, 0)
    lax.fori_loop(1, tiles + 1, body, 0, unroll=2)


def beside(field, tile, rows, centre):
    return behind(centre, field[tile - 1, rows, :]), ahead(centre, field[tile + 1, rows, :])


def flow_kernel(which, last_cond, height, keys, place_ref, weights_ref, *args):
    refs = dict(zip(keys, args))
    n_in = len(keys)
    surface_ref, low_ref, high_ref, base_ref, derived_ref = args[n_in : n_in + 5]
    scratch = (ELEV_MID, FIRST_MID, SECOND_MID, FLUX_A, FLUX_B)
    buf = dict(zip(scratch, args[n_in + 5 : n_in + 5 + len(scratch)]))
    buf.update((name, base_ref.at[k]) for k, name in enumerate(BASE_NAMES))
    buf.update((name, derived_ref.at[k]) for k, name in enumerate(DERIVED_NAMES))
    surface_buf, sem = args[n_in + 5 + len(scratch) :]
    tiles = base_ref.shape[1] - 2
    flow_places, _ = offsets(message(which, last_cond), tiles, height)
    static_places, _ = offsets(message(0, last_cond), tiles, height)
    count, need = halo_rows(height), rows_needed(height)

    zero = jnp.zeros((SPAN, LANES), jnp.float32)
    for name in (ELEV_MID, FLUX_B):
        buf[name][0, :, :] = zero
        buf[name][tiles + 1, :, :] = zero

    def load(head, tail, static_head, static_tail):
        def place(name, block, chunk, top, bottom, places):
            rows = count[name]
            where = pl.ds(places[name] + chunk * rows, rows)
            buf[name][block, OWN - rows : OWN, :] = top[where, :]
            buf[name][block, OWN + height : OWN + height + rows, :] = bottom[where, :]

        def body(tile, carry):
            block = tile + 1
            for name in FLOW:
                place(name, block, tile + (name in AHEAD), head, tail, flow_places)
            for name in (DEPTH, LIMITER):
                place(name, block, tile, static_head, static_tail, static_places)
            return carry

        for name in AHEAD:
            if name in FLOW:
                place(name, 0, 0, head, tail, flow_places)
        lax.fori_loop(0, tiles, body, 0, unroll=2)

    odd = place_ref[1]

    @pl.when(odd == 0)
    def _():
        load(refs[ACROSS], refs[CHIP], refs[STATIC_ACROSS], refs[STATIC_CHIP])

    @pl.when(odd == 1)
    def _():
        load(refs[CHIP], refs[ACROSS], refs[STATIC_CHIP], refs[STATIC_ACROSS])

    def outer(block, carry):
        for row in (OWN - 8, OWN + height):
            derive_rows(base_ref, derived_ref, block, row, DERIVED_NAMES)
        derive_rows(base_ref, derived_ref, block, OWN + height + 8, (KEEP,))
        return carry

    outer(0, 0)
    lax.fori_loop(1, tiles + 1, outer, 0, unroll=4)

    def starts(span_):
        return range(OWN + span_[0], OWN + span_[1] + 1, 8)

    def section(number):
        second = number % 2 == 0
        source = (ELEV_MID, FIRST_MID, SECOND_MID) if second else (ELEV, FIRST, SECOND)
        target = (ELEV, FIRST, SECOND) if second else (ELEV_MID, FIRST_MID, SECOND_MID)
        elev, first, vert = (buf[name] for name in source)
        final = number == 2 * STEPS

        def finish(name, at, rows, value):
            if second:
                value = 0.5 * (buf[name][at, rows, :] + value)
            if not (final and name == ELEV):
                buf[target[(ELEV, FIRST, SECOND).index(name)]][at, rows, :] = value
            return value

        def vertical(at):
            for row in starts(need[number][SECOND]):
                rows = slice(row, row + 8)
                here, after = elev[at, rows, :], elev[at + 1, rows, :]
                beyond = pltpu.roll(jnp.where(lane_index() < 2, after, here), LANES - 2, 1)
                kept = buf[KEEP_AHEAD][at, rows, :] * vert[at, rows, :] + buf[FORCE_B][at, rows, :]
                finish(SECOND, at, rows, kept - buf[WET_AHEAD][at, rows, :] * (beyond - here))

        def body(tile, carry):
            at = tile + 1
            for row in starts(need[number][ELEV]):
                rows, up, down = slice(row, row + 8), slice(row - 1, row + 7), slice(row + 1, row + 9)
                here, before = vert[at, rows, :], vert[at - 1, rows, :]
                back = pltpu.roll(jnp.where(lane_index() >= LANES - 2, before, here), 2, 1)
                gone = (first[at, down, :] - first[at, up, :]) + (here - back)
                value = finish(ELEV, at, rows, elev[at, rows, :] - buf[HALF][at, rows, :] * gone)
                if final:
                    surface_buf[row - OWN : row - OWN + 8, lanes_of(tile)] = value
            for row in starts(need[number][FIRST]):
                rows, up, down = slice(row, row + 8), slice(row - 1, row + 7), slice(row + 1, row + 9)
                kept = buf[KEEP][at, rows, :] * first[at, rows, :] + buf[FORCE_A][at, rows, :]
                finish(FIRST, at, rows, kept - buf[WET_DEPTH][at, rows, :] * (elev[at, down, :] - elev[at, up, :]))
            vertical(at)
            return carry

        vertical(0)
        lax.fori_loop(0, tiles, body, 0, unroll=UNROLL)

    def transports(step):
        def body(tile, carry):
            at = tile + 1
            for row in starts(need[-1][FIRST]):
                rows = slice(row, row + 8)
                inverse = buf[INVERSE][at, rows, :]
                vel_a = buf[FIRST][at, rows, :] * inverse
                vel_b = behind(buf[SECOND][at, rows, :], buf[SECOND][at - 1, rows, :]) * inverse
                energy = vel_a * vel_a + vel_b * vel_b
                factor = (transport_base + energy) / (1.0 + buf[LIMITER][at, rows, :] * energy)
                flux_a, flux_b = vel_a * factor, vel_b * factor
                if step:
                    flux_a = buf[FLUX_A][at, rows, :] + flux_a
                    flux_b = buf[FLUX_B][at, rows, :] + flux_b
                buf[FLUX_A][at, rows, :] = flux_a
                buf[FLUX_B][at, rows, :] = flux_b
            return carry

        lax.fori_loop(0, tiles, body, 0, unroll=UNROLL)

    for step in range(STEPS):
        section(2 * step + 1)
        section(2 * step + 2)
        if step == STEPS - 1:
            store = pltpu.make_async_copy(surface_buf, surface_ref.at[which], sem)
            store.start()
        transports(step)

    total = weights_ref[0]
    for other in range(1, weights_ref.shape[0]):
        total = total + weights_ref[other]
    scale = jnp.full((8, LANES), weights_ref[place_ref[0] + which], jnp.int32).astype(jnp.float32)
    scale = (-0.5 * morph_factor) * scale / jnp.full((8, LANES), total, jnp.int32).astype(jnp.float32)
    reach = height + ABOVE + BELOW
    begins = list(range(0, reach - 7, 8))
    if begins[-1] + 8 < reach:
        begins.append(reach - 8)

    def emit(out_ref, before, start):
        def body(local_tile, carry):
            at = start + local_tile + 1
            for begin in begins:
                row = OWN - ABOVE + begin
                rows, up, down = slice(row, row + 8), slice(row - 1, row + 7), slice(row + 1, row + 9)
                left, right = beside(buf[FLUX_B], at, rows, buf[FLUX_B][at, rows, :])
                change = (buf[FLUX_A][at, down, :] - buf[FLUX_A][at, up, :]) + (right - left)
                where = pl.ds(local_tile * reach + begin, 8)
                piece = scale * change
                if before is not None:
                    piece = before[where, :] + piece
                out_ref[where, :] = piece
            return carry

        lax.fori_loop(0, tiles // 2, body, 0, unroll=UNROLL)

    emit(low_ref, refs.get(LOW), 0)
    emit(high_ref, refs.get(HIGH), tiles // 2)
    store.wait()


FIELD = 8


def faces_kernel(last, place_ref, bed_ref, diffuse_ref, across_ref, chip_ref, _, faces_ref, wide):
    height, tiles = bed_ref.shape[0], bed_ref.shape[1] // LANES
    places, _ = offsets(message(last, last), tiles, height)
    count = halo_rows(height)
    zero = jnp.zeros(wide.shape[1:], jnp.float32)
    wide[0, :, :] = zero
    wide[tiles + 1, :, :] = zero

    def load(head, tail):
        def body(tile, carry):
            for name, dst, block, ref in ((BED, faces_ref.at[0], tile, bed_ref), (DIFFUSIVITY, wide, tile + 1, diffuse_ref)):
                rows = count[name]
                where = pl.ds(places[name] + tile * rows, rows)
                dst[block, FIELD - rows : FIELD, :] = head[where, :]
                for row in range(0, height, 8):
                    dst[block, FIELD + row : FIELD + row + 8, :] = ref[row : row + 8, lanes_of(tile)]
                dst[block, FIELD + height : FIELD + height + rows, :] = tail[where, :]
            return carry

        lax.fori_loop(0, tiles, body, 0, unroll=2)

    odd = place_ref[1]

    @pl.when(odd == 0)
    def _():
        load(across_ref, chip_ref)

    @pl.when(odd == 1)
    def _():
        load(chip_ref, across_ref)

    def face(here, there):
        both = here + there
        return jnp.where(both > 0.0, slope_coeff * here * there / both, 0.0)

    def body(tile, carry):
        at = tile + 1
        for row in range(FIELD, FIELD + height + 1, 8):
            rows, up = slice(row, row + 8), slice(row - 1, row + 7)
            here = wide[at, rows, :]
            left, right = beside(wide, at, rows, here)
            faces_ref[1, tile, up, :] = face(wide[at, up, :], here)
            faces_ref[2, tile, rows, :] = face(here, right)
            faces_ref[3, tile, rows, :] = face(here, left)
        return carry

    lax.fori_loop(0, tiles, body, 0, unroll=2)


def moment_kernel(faces_ref, low_ref, low_other_ref, high_ref, high_other_ref, rhs_ref, image_ref, moments_ref, field, image):
    tiles, height = rhs_ref.shape[:2]
    reach = height + ABOVE + BELOW
    zero = jnp.zeros(field.shape[1:], jnp.float32)
    for scratch in (field, image):
        scratch[0, :, :] = zero
        scratch[tiles + 1, :, :] = zero
    begins = list(range(0, reach - 7, 8))
    if begins[-1] + 8 < reach:
        begins.append(reach - 8)

    def add(mine, other, start):
        def body(local_tile, carry):
            for begin in begins:
                where = pl.ds(local_tile * reach + begin, 8)
                rows = slice(FIELD - ABOVE + begin, FIELD - ABOVE + begin + 8)
                tile = start + local_tile
                field[tile + 1, rows, :] = faces_ref[0, tile, rows, :] + (mine[where, :] + other[where, :])
            return carry

        lax.fori_loop(0, tiles // 2, body, 0, unroll=True)

    add(low_ref, low_other_ref, 0)
    add(high_ref, high_other_ref, tiles // 2)

    def apply(tile, carry):
        at = tile + 1
        square, first = carry
        for row in range(FIELD, FIELD + height + 1, 8):
            rows, up, down = slice(row, row + 8), slice(row - 1, row + 7), slice(row + 1, row + 9)
            x = field[at, rows, :]
            left, right = beside(field, at, rows, x)
            gap_down, gap_right = x - field[at, down, :], x - right
            flow_down, flow_right = faces_ref[1, tile, rows, :] * gap_down, faces_ref[2, tile, rows, :] * gap_right
            result = (flow_down + faces_ref[1, tile, up, :] * (x - field[at, up, :])) + (
                flow_right + faces_ref[3, tile, rows, :] * (x - left)
            )
            image[at, rows, :] = result
            if row < FIELD + height:
                rhs_ref[tile, row - FIELD : row - FIELD + 8, :] = x
                image_ref[tile, row - FIELD : row - FIELD + 8, :] = result
                square = square + x * x
                first = first + (flow_down * gap_down + flow_right * gap_right)
        return square, first

    zero = jnp.zeros((8, LANES), jnp.float32)
    square, first = lax.fori_loop(0, tiles, apply, (zero, zero), unroll=True)

    def again(tile, carry):
        at = tile + 1
        second, third = carry
        for row in range(FIELD, FIELD + height, 8):
            rows, down = slice(row, row + 8), slice(row + 1, row + 9)
            w = image[at, rows, :]
            gap_down, gap_right = w - image[at, down, :], w - ahead(w, image[at + 1, rows, :])
            second = second + w * w
            third = third + (
                faces_ref[1, tile, rows, :] * (gap_down * gap_down) + faces_ref[2, tile, rows, :] * (gap_right * gap_right)
            )
        return second, third

    second, third = lax.fori_loop(0, tiles, again, (zero, zero), unroll=True)
    for slot, value in enumerate((square, first, second, third)):
        moments_ref[slot : slot + 1, :] = jnp.sum(value, axis=0, keepdims=True)
    moments_ref[4:8, :] = jnp.zeros((4, LANES), jnp.float32)


def final_kernel(rhs_ref, image_ref, *args):
    moments, (out_ref,) = args[:-1], args[-1:]
    total = moments[0][...]
    for part in moments[1:]:
        total = total + part[...]
    total = jnp.sum(total, axis=1, keepdims=True)
    norm, first, second, third = (total[slot : slot + 1, :] for slot in range(4))
    alpha = norm / (norm + first)
    theta = first / norm
    spread_ = second - theta * first
    curve = third - 2.0 * theta * second + theta * theta * first
    ratio = alpha * alpha * spread_ / norm
    beta = spread_ / (spread_ + curve - alpha * spread_ * (spread_ / norm))
    on_rhs = jnp.broadcast_to(alpha + beta * (alpha * theta + ratio), (8, LANES))
    on_image = jnp.broadcast_to(beta * alpha, (8, LANES))
    tiles, height = rhs_ref.shape[:2]

    def body(tile, carry):
        for row in range(0, height, 8):
            rows = slice(row, row + 8)
            out_ref[rows, lanes_of(tile)] = on_rhs * rhs_ref[tile, rows, :] - on_image * image_ref[tile, rows, :]
        return carry

    lax.fori_loop(0, tiles, body, 0, unroll=4)


SMEM = pl.BlockSpec(memory_space=pltpu.SMEM)
PARAMS = dict(vmem_limit_bytes=32 * 1024 * 1024)


def cost(flops, moved):
    return pl.CostEstimate(flops=flops, bytes_accessed=moved, transcendentals=0)


def swap_chip(x, count):
    return lax.ppermute(x, "space", [(i, i ^ 1) for i in range(count)])


def swap_across(x, count):
    pairs = [(i, i + 1) for i in range(1, count - 1, 2)]
    return lax.ppermute(x, "space", pairs + [(b, a) for a, b in pairs])


def phases_of(count):
    bits = [1 << k for k in range(count.bit_length() - 1)]
    out = [bits[:1]]
    for k in range(1, len(bits), 2):
        pair = bits[k : k + 2]
        out.append([pair[0]] if len(pair) == 1 else [pair[0], pair[1], pair[0] + pair[1]])
    return out


def local(flow, forcing, wet, depth, limiter, weights, bed, diffusivity):
    here, _, height, width = flow.shape
    bed_here, diffuse_here = bed, diffusivity
    flow, forcing, wet, depth, limiter, bed, diffusivity = (
        pltpu.with_memory_space_constraint(v, pltpu.HBM) for v in (flow, forcing, wet, depth, limiter, bed, diffusivity)
    )
    tiles = width // LANES
    strips, groups = lax.axis_size("space"), lax.axis_size("cond")
    place = jnp.stack([lax.axis_index("cond") * here, lax.axis_index("space") % 2]).astype(jnp.int32)
    reach = height + ABOVE + BELOW

    last = here - 1
    local_vmem = pl.BlockSpec(memory_space=pltpu.VMEM)
    anywhere = pl.BlockSpec(memory_space=pltpu.HBM)
    base_shape = jax.ShapeDtypeStruct((len(BASE_NAMES), tiles + 2, SPAN, LANES), jnp.float32)
    derived_shape = jax.ShapeDtypeStruct((len(DERIVED_NAMES), tiles + 2, SPAN, LANES), jnp.float32)

    across, chip, base, derived = [], [], [], []
    for which in range(here):
        arrays = {FLOW_IN: flow, FORCING: forcing, WET: wet, DEPTH: depth, LIMITER: limiter}
        if which == last:
            arrays.update({BED: bed, DIFFUSIVITY: diffusivity})
        keys = tuple(arrays)
        size = offsets(message(which, last), tiles, height)[1]
        shape = jax.ShapeDtypeStruct((size, LANES), jnp.float32)
        held = [pltpu.VMEM(v.shape[1:] if k in (FLOW_IN, FORCING, WET) else v.shape, v.dtype) for k, v in arrays.items()]
        out = pl.pallas_call(
            functools.partial(prepare_kernel, which, last, keys),
            out_shape=(shape, shape, base_shape) + (derived_shape,) * bool(which),
            in_specs=[SMEM] + [anywhere] * len(keys) + [pl.BlockSpec(memory_space=pl.ANY)] * bool(which),
            out_specs=(local_vmem,) * (3 + bool(which)),
            scratch_shapes=held
            + [pltpu.VMEM((tiles + 2, height, LANES), jnp.float32)] * 2
            + [pltpu.SemaphoreType.DMA((len(keys),))],
            compiler_params=pltpu.CompilerParams(**PARAMS),
            cost_estimate=cost(1000, 8 * height * width * 4 + size * LANES * 8),
            name=f"prepare{which}",
        )(place, *arrays.values(), *derived[-1:])
        across.append(swap_across(out[0], strips))
        chip.append(swap_chip(out[1], strips))
        base.append(out[2])
        if which:
            derived.append(out[3])
        else:
            derived.append(
                pl.pallas_call(
                    functools.partial(derive_kernel, height=height),
                    out_shape=derived_shape,
                    in_specs=[local_vmem],
                    out_specs=local_vmem,
                    compiler_params=pltpu.CompilerParams(**PARAMS),
                    cost_estimate=cost(1000, 7 * height * width * 4),
                    name="derive",
                )(out[2])
            )

    surface_shape = jax.ShapeDtypeStruct((here, height, width), jnp.float32)
    half_shape = jax.ShapeDtypeStruct((tiles // 2 * reach, LANES), jnp.float32)
    surface = low = high = None
    for which in range(here):
        arrays = {ACROSS: across[which], CHIP: chip[which], STATIC_ACROSS: across[0], STATIC_CHIP: chip[0]}
        if which:
            arrays.update({LOW: low, HIGH: high})
        arrays.update({BASE: base[which], DERIVED: derived[which]})
        specs = [local_vmem] * len(arrays)
        aliases = {len(arrays): 3, len(arrays) + 1: 4}
        if which:
            arrays[SURFACE] = surface
            specs.append(anywhere)
            aliases[1 + len(arrays)] = 0
        keys = tuple(arrays)
        surface, low, high, _, _ = pl.pallas_call(
            functools.partial(flow_kernel, which, last, height, keys),
            out_shape=(surface_shape, half_shape, half_shape, base_shape, derived_shape),
            in_specs=[SMEM, SMEM] + specs,
            out_specs=(anywhere,) + (local_vmem,) * 4,
            scratch_shapes=[pltpu.VMEM((tiles + 2, SPAN, LANES), jnp.float32)] * 5
            + [pltpu.VMEM((height, width), jnp.float32), pltpu.SemaphoreType.DMA],
            input_output_aliases=aliases,
            compiler_params=pltpu.CompilerParams(**PARAMS),
            cost_estimate=cost(2 * STEPS * 40 * 40 * width, 8 * height * width * 4),
            name=f"flow{which}",
        )(place, weights, *arrays.values())

    faces = pl.pallas_call(
        functools.partial(faces_kernel, last),
        out_shape=jax.ShapeDtypeStruct((4, tiles, height + 24, LANES), jnp.float32),
        in_specs=[SMEM] + [local_vmem] * 4 + [pl.BlockSpec(memory_space=pl.ANY)],
        out_specs=local_vmem,
        scratch_shapes=[pltpu.VMEM((tiles + 2, height + 24, LANES), jnp.float32)],
        compiler_params=pltpu.CompilerParams(**PARAMS),
        cost_estimate=cost(60 * height * width, 8 * height * width * 4),
        name="faces",
    )(place, bed_here, diffuse_here, across[last], chip[last], low)

    bits = [1 << k for k in range(groups.bit_length() - 1)]
    for k, bit in enumerate(bits):
        low_other = lax.ppermute(low, "cond", [(i, i ^ bit) for i in range(groups)])
        flip = bits[-1 - k]
        high_other = lax.ppermute(high, "cond", [(i, i ^ flip) for i in range(groups)])
        if k + 1 < len(bits):
            low, high = low + low_other, high + high_other

    block = jax.ShapeDtypeStruct((tiles, height, LANES), jnp.float32)
    small = jax.ShapeDtypeStruct((8, LANES), jnp.float32)
    wide = pltpu.VMEM((tiles + 2, height + 24, LANES), jnp.float32)
    rhs, image, moments = pl.pallas_call(
        moment_kernel,
        out_shape=(block, block, small),
        in_specs=[local_vmem] * 5,
        out_specs=(local_vmem,) * 3,
        scratch_shapes=[wide] * 2,
        compiler_params=pltpu.CompilerParams(**PARAMS),
        cost_estimate=cost(60 * height * width, 8 * height * width * 4),
        name="moments",
    )(faces, low, low_other, high, high_other)

    phases = phases_of(strips)
    for k, phase in enumerate(phases):
        others = [lax.ppermute(moments, "space", [(i, i ^ m) for i in range(strips)]) for m in phase]
        if k + 1 < len(phases):
            for other in others:
                moments = moments + other

    terms = [moments] + others
    bed_new = pl.pallas_call(
        final_kernel,
        out_shape=jax.ShapeDtypeStruct((height, width), jnp.float32),
        in_specs=[local_vmem] * (2 + len(terms)),
        out_specs=local_vmem,
        compiler_params=pltpu.CompilerParams(**PARAMS),
        cost_estimate=cost(3 * height * width, 3 * height * width * 4),
        name="final",
    )(rhs, image, *terms)
    return (surface, bed_new)


def solution(mesh):
    in_specs = (
        P("cond", None, "space", None),
        P("cond", None, "space", None),
        P("cond", "space", None),
        P("space", None),
        P("space", None),
        P(),
        P("space", None),
        P("space", None),
    )
    out_specs = (P("cond", "space", None), P("space", None))
    return jax.shard_map(local, mesh=mesh, in_specs=in_specs, out_specs=out_specs, check_vma=False)
```

time: 73.5 us -> 48.4 us (0.66)
  Pallas kernels: 35.5 us -> 19.6 us
  local copies, waits for them, and re-layouts: 4.96 us -> 0.02 us
  starting transfers between devices: 22.9 us -> 19.3 us
    pallas_call x5 -> x7, Pallas kernels: 34.6 us -> 18.7 us  [the longest x2 10.6 us: local(): pl.pallas_call(functools.partial(flow_kernel, which, last, height, keys),...]
    unnamed x20 -> x6, local copies, waits for them, and re-layouts: 4.96 us -> 0.02 us
    ppermute x4, starting transfers between devices: 7.91 us -> 4.46 us  [local(): lax.ppermute(moments, 'space', [(i, i ^ m) for i in range(strips)])]
    ppermute x2, waiting for transfers between devices: 2.69 us -> 1.56 us  [local(): low_other = lax.ppermute(low, 'cond', [(i, i ^ bit) for i in range(groups)])]
  transfers between devices with their start and end apart: 12 -> 12, of which waited for: 6 -> 7; matrix products, arithmetic and copies ran while one was open for 0% -> 0% of each run, Pallas kernels for 21% -> 22%
where the time goes in v2:
time: 48.4 us; the launch traced here: 48.2 us
  Pallas kernels  19.6 us (40%)
  starting transfers between devices  19.3 us (40%)
  waiting for transfers between devices  8.51 us (18%)
  between operations  0.77 us (2%)
    pallas_call x2, Pallas kernels, local(): pl.pallas_call(functools.partial(flow_kernel, which, last, height, keys),...  10.6 us
    ppermute x2, starting transfers between devices, swap_chip(): return lax.ppermute(x, 'space', [(i, i ^ 1) for i in range(count)])  7.41 us
    pallas_call x2, Pallas kernels, local(): pl.pallas_call(functools.partial(prepare_kernel, which, last, keys), out_...  5.78 us
    ppermute x4, waiting for transfers between devices, local(): lax.ppermute(moments, 'space', [(i, i ^ m) for i in range(strips)])  4.81 us
    ppermute x4, starting transfers between devices, local(): lax.ppermute(moments, 'space', [(i, i ^ m) for i in range(strips)])  4.46 us
    ppermute x2, starting transfers between devices, local(): lax.ppermute(high, 'cond', [(i, i ^ flip) for i in range(groups)])  3.14 us
    ppermute x2, starting transfers between devices, local(): low_other = lax.ppermute(low, 'cond', [(i, i ^ bit) for i in range(groups)])  2.85 us
    ppermute x2, waiting for transfers between devices, local(): lax.ppermute(high, 'cond', [(i, i ^ flip) for i in range(groups)])  2.13 us
  transfers between devices with their start and end apart: 12, of which 7 were waited for; matrix products, arithmetic and copies ran while one was open for 0% of the time, Pallas kernels for 22%

profile of v2, /device:TPU:0, one launch (start us, length us, event | category | flops | bytes accessed | tf_op | source)
XLA Modules:
  0.0 48.2 jit_solution(2627506380666766036)
XLA Ops:
  0.6 0.1 pad_add_fusion.place_ref
  0.7 2.5 %prepare0.1 = (f32[1144,128]{1,0:T(8,128)S(1)}, f32[1144,128]{1,0:T(8,128)S(1)}, f32[8,18,64,128]{3,2,1,0:T(8,128)S(1)}) custom-call(s32[2]{0:T(128)S(1)} %pad_add_fusion.place_ref, f32[2,3,16,2048]{3,2,1,0:T(8,128)} %args_0_.6, f32[2,2,16,2048]{3,2,1,0:T(8,128)} %args_1_.6, s32[2,16,2048]{2,1,0:T(8,128)} %args_2_.6, f32[16,2048]{1,0:T(8,128)} %args_3_.6, ...), custom_call_target="tpu_custom_call" | custom-call | flops 1000 | bytes 2220032 | tf_op jit(solution)/shard_map/prepare0/pallas_call | solution.py:583
  3.2 0.7 %collective-permute-start.2 = (f32[1144,128]{1,0:T(8,128)S(1)}, f32[1144,128]{1,0:T(8,128)S(1)}, u32[]{:S(2)}, u32[]{:S(2)}) collective-permute-start(f32[1144,128]{1,0:T(8,128)S(1)} %get-tuple-element.21), channel_id=1, source_target_pairs={{1,2},{3,4},{5,6},{2,1},{4,3},{6,5},{9,10},{11,12},{13,14},{10,9},... | collective-permute-start | bytes 1757192 | tf_op jit(solution)/shard_map/ppermute | solution.py:545
  3.9 4.4 %collective-permute-start.3 = (f32[1144,128]{1,0:T(8,128)S(1)}, f32[1144,128]{1,0:T(8,128)S(1)}, u32[]{:S(2)}, u32[]{:S(2)}) collective-permute-start(f32[1144,128]{1,0:T(8,128)S(1)} %get-tuple-element.22), channel_id=1, source_target_pairs={{0,1},{1,0},{2,3},{3,2},{4,5},{5,4},{6,7},{7,6},{8,9},{9,8},{10,11... | collective-permute-start | bytes 1757192 | tf_op jit(solution)/shard_map/ppermute | solution.py:540
  8.4 0.7 %derive.1.args_7_.args_5_ = f32[5,18,64,128]{3,2,1,0:T(8,128)S(1)} custom-call(f32[8,18,64,128]{3,2,1,0:T(8,128)S(1)} %get-tuple-element.18.base_ref.args_4_), custom_call_target="tpu_custom_call" | custom-call | flops 1000 | bytes 917504 | tf_op jit(solution)/shard_map/derive/pallas_call | solution.py:602
  9.1 0.0 copy-start.2
  9.1 3.3 %prepare1.1 = (f32[1016,128]{1,0:T(8,128)S(1)}, f32[1016,128]{1,0:T(8,128)S(1)}, f32[8,18,64,128]{3,2,1,0:T(8,128)S(1)}, f32[5,18,64,128]{3,2,1,0:T(8,128)S(1)}) custom-call(s32[2]{0:T(128)S(1)} %pad_add_fusion.place_ref, f32[2,3,16,2048]{3,2,1,0:T(8,128)} %args_0_.6, f32[2,2,16,2048]{3,2,1,0:T(8,128)} %args_1_.6, s32[2,16,2048]{2,1,0:T(8,128)} %args_2_.6, ...), custom_call_target="tpu_custom_call" | custom-call | flops 1000 | bytes 2088960 | tf_op jit(solution)/shard_map/prepare1/pallas_call | solution.py:583
  12.4 0.7 %collective-permute-start = (f32[1016,128]{1,0:T(8,128)S(1)}, f32[1016,128]{1,0:T(8,128)S(1)}, u32[]{:S(2)}, u32[]{:S(2)}) collective-permute-start(f32[1016,128]{1,0:T(8,128)S(1)} %get-tuple-element.19), channel_id=1, source_target_pairs={{1,2},{3,4},{5,6},{2,1},{4,3},{6,5},{9,10},{11,12},{13,14},{10,9},... | collective-permute-start | bytes 1560584 | tf_op jit(solution)/shard_map/ppermute | solution.py:545
  13.1 3.0 %collective-permute-start.1 = (f32[1016,128]{1,0:T(8,128)S(1)}, f32[1016,128]{1,0:T(8,128)S(1)}, u32[]{:S(2)}, u32[]{:S(2)}) collective-permute-start(f32[1016,128]{1,0:T(8,128)S(1)} %get-tuple-element.20), channel_id=1, source_target_pairs={{0,1},{1,0},{2,3},{3,2},{4,5},{5,4},{6,7},{7,6},{8,9},{9,8},{10,11... | collective-permute-start | bytes 1560584 | tf_op jit(solution)/shard_map/ppermute | solution.py:540
  16.0 0.0 collective-permute-done.2.args_0_.args_2_
  16.0 0.0 collective-permute-done.3.args_1_.args_3_
  16.0 0.0 copy-done.2
  16.1 5.3 %flow0.1 = (f32[2,16,2048]{2,1,0:T(8,128)}, f32[152,128]{1,0:T(8,128)S(1)}, f32[152,128]{1,0:T(8,128)S(1)}, f32[8,18,64,128]{3,2,1,0:T(8,128)S(1)}, f32[5,18,64,128]{3,2,1,0:T(8,128)S(1)}) custom-call(s32[2]{0:T(128)S(1)} %pad_add_fusion.place_ref, s32[8]{0:T(128)S(1)} %copy-done.2, ...), custom_call_target="tpu_custom_call", output_to_operand_aliasing={{3}: (6, {}), {4}: (7, {})} | custom-call | flops 26214400 | bytes 1048576 | tf_op jit(solution)/shard_map/flow0/pallas_call | solution.py:628
  21.3 0.0 collective-permute-done.args_0_.across_ref
  21.3 0.0 collective-permute-done.1.args_1_.chip_ref
  21.4 0.0 copy-start
  21.4 0.0 copy-start.1
  21.4 5.3 %flow1.1 = (f32[2,16,2048]{2,1,0:T(8,128)}, f32[152,128]{1,0:T(8,128)S(1)}, f32[152,128]{1,0:T(8,128)S(1)}, f32[8,18,64,128]{3,2,1,0:T(8,128)S(1)}, f32[5,18,64,128]{3,2,1,0:T(8,128)S(1)}) custom-call(s32[2]{0:T(128)S(1)} %pad_add_fusion.place_ref, s32[8]{0:T(128)S(1)} %copy-done.2, ...), custom_call_target="tpu_custom_call", output_to_operand_aliasing={{3}: (8, {}), {4}: (9, {}), {0}: (10, {})} | custom-call | flops 26214400 | bytes 1048576 | tf_op jit(solution)/shard_map/flow1/pallas_call | solution.py:628
  26.7 1.6 %collective-permute-start.6 = (f32[152,128]{1,0:T(8,128)S(1)}, f32[152,128]{1,0:T(8,128)S(1)}, u32[]{:S(2)}, u32[]{:S(2)}) collective-permute-start(f32[152,128]{1,0:T(8,128)S(1)} %get-tuple-element.30), channel_id=1, source_target_pairs={{0,16},{8,24},{16,0},{24,8},{1,17},{9,25},{17,1},{25,9},{2,18},{10... | collective-permute-start | bytes 233480 | tf_op jit(solution)/shard_map/ppermute | solution.py:656
  28.3 1.5 %collective-permute-start.4 = (f32[152,128]{1,0:T(8,128)S(1)}, f32[152,128]{1,0:T(8,128)S(1)}, u32[]{:S(2)}, u32[]{:S(2)}) collective-permute-start(f32[152,128]{1,0:T(8,128)S(1)} %get-tuple-element.29._), channel_id=1, source_target_pairs={{0,8},{8,0},{16,24},{24,16},{1,9},{9,1},{17,25},{25,17},{2,10},{10... | collective-permute-start | bytes 233480 | tf_op jit(solution)/shard_map/ppermute | solution.py:654
  29.8 1.7 %collective-permute-done.6 = f32[152,128]{1,0:T(8,128)S(1)} collective-permute-done((f32[152,128]{1,0:T(8,128)S(1)}, f32[152,128]{1,0:T(8,128)S(1)}, u32[]{:S(2)}, u32[]{:S(2)}) %collective-permute-start.6) | collective-permute-done | bytes 77856 | tf_op jit(solution)/shard_map/ppermute | solution.py:656
  31.5 1.6 %collective-permute-start.7 = (f32[152,128]{1,0:T(8,128)S(1)}, f32[152,128]{1,0:T(8,128)S(1)}, u32[]{:S(2)}, u32[]{:S(2)}) collective-permute-start(f32[152,128]{1,0:T(8,128)S(1)} %add.15.high_ref), channel_id=1, source_target_pairs={{0,8},{8,0},{16,24},{24,16},{1,9},{9,1},{17,25},{25,17},{2,10},{10... | collective-permute-start | bytes 233480 | tf_op jit(solution)/shard_map/ppermute | solution.py:656
  33.1 0.2 collective-permute-done.4
  33.3 1.4 %collective-permute-start.5 = (f32[152,128]{1,0:T(8,128)S(1)}, f32[152,128]{1,0:T(8,128)S(1)}, u32[]{:S(2)}, u32[]{:S(2)}) collective-permute-start(f32[152,128]{1,0:T(8,128)S(1)} %add.14.low_ref), channel_id=1, source_target_pairs={{0,16},{8,24},{16,0},{24,8},{1,17},{9,25},{17,1},{25,9},{2,18},{10... | collective-permute-start | bytes 233480 | tf_op jit(solution)/shard_map/ppermute | solution.py:654
  34.7 0.0 copy-done
  34.7 0.0 copy-done.1
  34.7 1.4 %faces.1.faces_ref = f32[4,16,40,128]{3,2,1,0:T(8,128)S(1)} custom-call(s32[2]{0:T(128)S(1)} %pad_add_fusion.place_ref, f32[16,2048]{1,0:T(8,128)S(1)} %copy-done, f32[16,2048]{1,0:T(8,128)S(1)} %copy-done.1, f32[1016,128]{1,0:T(8,128)S(1)} %collective-permute-done.args_0_.across_ref, f32[1016,128]{1,0:T(8,128)S(1)} %collective-permute-done.1.args_1_.chip_ref, ...), custom_call_target="tpu_custom_call" | custom-call | flops 1966080 | bytes 1048576 | tf_op jit(solution)/shard_map/faces/pallas_call | solution.py:641
  36.1 0.4 collective-permute-done.7.high_other_ref
  36.5 1.3 %collective-permute-done.5.low_other_ref = f32[152,128]{1,0:T(8,128)S(1)} collective-permute-done((f32[152,128]{1,0:T(8,128)S(1)}, f32[152,128]{1,0:T(8,128)S(1)}, u32[]{:S(2)}, u32[]{:S(2)}) %collective-permute-start.5) | collective-permute-done | bytes 77856 | tf_op jit(solution)/shard_map/ppermute | solution.py:654
  37.8 0.3 moments.1
  38.1 0.1 collective-permute-start.8
  38.2 1.2 %collective-permute-done.8 = f32[8,128]{1,0:T(8,128)S(1)} collective-permute-done((f32[8,128]{1,0:T(8,128)S(1)}, f32[8,128]{1,0:T(8,128)S(1)}, u32[]{:S(2)}, u32[]{:S(2)}) %collective-permute-start.8) | collective-permute-done | bytes 4128 | tf_op jit(solution)/shard_map/ppermute | solution.py:676
  39.3 3.5 %collective-permute-start.11 = (f32[8,128]{1,0:T(8,128)S(1)}, f32[8,128]{1,0:T(8,128)S(1)}, u32[]{:S(2)}, u32[]{:S(2)}) collective-permute-start(f32[8,128]{1,0:T(8,128)S(1)} %add.16.args_0_), channel_id=1, source_target_pairs={{0,6},{1,7},{2,4},{3,5},{4,2},{5,3},{6,0},{7,1},{8,14},{9,15},{10,... | collective-permute-start | bytes 12296 | tf_op jit(solution)/shard_map/ppermute | solution.py:676
  42.9 0.4 collective-permute-start.10
  43.2 0.5 collective-permute-start.9
  43.7 1.0 %collective-permute-done.11.args_3_ = f32[8,128]{1,0:T(8,128)S(1)} collective-permute-done((f32[8,128]{1,0:T(8,128)S(1)}, f32[8,128]{1,0:T(8,128)S(1)}, u32[]{:S(2)}, u32[]{:S(2)}) %collective-permute-start.11) | collective-permute-done | bytes 4128 | tf_op jit(solution)/shard_map/ppermute | solution.py:676
  44.7 2.6 %collective-permute-done.10.args_2_ = f32[8,128]{1,0:T(8,128)S(1)} collective-permute-done((f32[8,128]{1,0:T(8,128)S(1)}, f32[8,128]{1,0:T(8,128)S(1)}, u32[]{:S(2)}, u32[]{:S(2)}) %collective-permute-start.10) | collective-permute-done | bytes 4128 | tf_op jit(solution)/shard_map/ppermute | solution.py:676
  47.4 0.0 collective-permute-done.9.args_1_
  47.4 0.8 %final.1 = f32[16,2048]{1,0:T(8,128)} custom-call(f32[16,16,128]{2,1,0:T(8,128)S(1)} %get-tuple-element.31.rhs_ref, f32[16,16,128]{2,1,0:T(8,128)S(1)} %get-tuple-element.32.image_ref, f32[8,128]{1,0:T(8,128)S(1)} %add.16.args_0_, f32[8,128]{1,0:T(8,128)S(1)} %collective-permute-done.9.args_1_, f32[8,128]{1,0:T(8,128)S(1)} %collective-permute-done.10.args_2_, ...), custom_call_target="tpu_custom_call" | custom-call | flops 98304 | bytes 393216 | tf_op jit(solution)/shard_map/final/pallas_call | solution.py:682
  (3 shorter events, 0.0 us)
Async XLA Ops:
  3.2 12.8 %collective-permute-start.2 = (f32[1144,128]{1,0:T(8,128)S(1)}, f32[1144,128]{1,0:T(8,128)S(1)}, u32[]{:S(2)}, u32[]{:S(2)}) collective-permute-start(f32[1144,128]{1,0:T(8,128)S(1)} %get-tuple-element.21), channel_id=1, source_target_pairs={{1,2},{3,4},{5,6},{2,1},{4,3},{6,5},{9,10},{11,12},{13,14},{10,9},... | collective-permute-start | bytes 1757192 | tf_op jit(solution)/shard_map/ppermute | solution.py:545
  3.9 12.1 %collective-permute-start.3 = (f32[1144,128]{1,0:T(8,128)S(1)}, f32[1144,128]{1,0:T(8,128)S(1)}, u32[]{:S(2)}, u32[]{:S(2)}) collective-permute-start(f32[1144,128]{1,0:T(8,128)S(1)} %get-tuple-element.22), channel_id=1, source_target_pairs={{0,1},{1,0},{2,3},{3,2},{4,5},{5,4},{6,7},{7,6},{8,9},{9,8},{10,11... | collective-permute-start | bytes 1757192 | tf_op jit(solution)/shard_map/ppermute | solution.py:540
  9.1 7.0 %copy-start.2 = (s32[8]{0:T(128)S(1)}, s32[8]{0:T(128)}, u32[]{:S(2)}) copy-start(s32[8]{0:T(128)} %weights_ref.3) | copy-start | bytes 100
  12.4 9.0 %collective-permute-start = (f32[1016,128]{1,0:T(8,128)S(1)}, f32[1016,128]{1,0:T(8,128)S(1)}, u32[]{:S(2)}, u32[]{:S(2)}) collective-permute-start(f32[1016,128]{1,0:T(8,128)S(1)} %get-tuple-element.19), channel_id=1, source_target_pairs={{1,2},{3,4},{5,6},{2,1},{4,3},{6,5},{9,10},{11,12},{13,14},{10,9},... | collective-permute-start | bytes 1560584 | tf_op jit(solution)/shard_map/ppermute | solution.py:545
  13.1 8.3 %collective-permute-start.1 = (f32[1016,128]{1,0:T(8,128)S(1)}, f32[1016,128]{1,0:T(8,128)S(1)}, u32[]{:S(2)}, u32[]{:S(2)}) collective-permute-start(f32[1016,128]{1,0:T(8,128)S(1)} %get-tuple-element.20), channel_id=1, source_target_pairs={{0,1},{1,0},{2,3},{3,2},{4,5},{5,4},{6,7},{7,6},{8,9},{9,8},{10,11... | collective-permute-start | bytes 1560584 | tf_op jit(solution)/shard_map/ppermute | solution.py:540
  21.4 13.3 %copy-start = (f32[16,2048]{1,0:T(8,128)S(1)}, f32[16,2048]{1,0:T(8,128)}, u32[]{:S(2)}) copy-start(f32[16,2048]{1,0:T(8,128)} %bed_ref.1) | copy-start | bytes 393220
  21.4 13.3 %copy-start.1 = (f32[16,2048]{1,0:T(8,128)S(1)}, f32[16,2048]{1,0:T(8,128)}, u32[]{:S(2)}) copy-start(f32[16,2048]{1,0:T(8,128)} %diffuse_ref.1) | copy-start | bytes 393220
  26.7 4.8 %collective-permute-start.6 = (f32[152,128]{1,0:T(8,128)S(1)}, f32[152,128]{1,0:T(8,128)S(1)}, u32[]{:S(2)}, u32[]{:S(2)}) collective-permute-start(f32[152,128]{1,0:T(8,128)S(1)} %get-tuple-element.30), channel_id=1, source_target_pairs={{0,16},{8,24},{16,0},{24,8},{1,17},{9,25},{17,1},{25,9},{2,18},{10... | collective-permute-start | bytes 233480 | tf_op jit(solution)/shard_map/ppermute | solution.py:656
  28.3 5.0 %collective-permute-start.4 = (f32[152,128]{1,0:T(8,128)S(1)}, f32[152,128]{1,0:T(8,128)S(1)}, u32[]{:S(2)}, u32[]{:S(2)}) collective-permute-start(f32[152,128]{1,0:T(8,128)S(1)} %get-tuple-element.29._), channel_id=1, source_target_pairs={{0,8},{8,0},{16,24},{24,16},{1,9},{9,1},{17,25},{25,17},{2,10},{10... | collective-permute-start | bytes 233480 | tf_op jit(solution)/shard_map/ppermute | solution.py:654
  31.5 4.9 %collective-permute-start.7 = (f32[152,128]{1,0:T(8,128)S(1)}, f32[152,128]{1,0:T(8,128)S(1)}, u32[]{:S(2)}, u32[]{:S(2)}) collective-permute-start(f32[152,128]{1,0:T(8,128)S(1)} %add.15.high_ref), channel_id=1, source_target_pairs={{0,8},{8,0},{16,24},{24,16},{1,9},{9,1},{17,25},{25,17},{2,10},{10... | collective-permute-start | bytes 233480 | tf_op jit(solution)/shard_map/ppermute | solution.py:656
  33.3 4.5 %collective-permute-start.5 = (f32[152,128]{1,0:T(8,128)S(1)}, f32[152,128]{1,0:T(8,128)S(1)}, u32[]{:S(2)}, u32[]{:S(2)}) collective-permute-start(f32[152,128]{1,0:T(8,128)S(1)} %add.14.low_ref), channel_id=1, source_target_pairs={{0,16},{8,24},{16,0},{24,8},{1,17},{9,25},{17,1},{25,9},{2,18},{10... | collective-permute-start | bytes 233480 | tf_op jit(solution)/shard_map/ppermute | solution.py:654
  38.1 1.2 %collective-permute-start.8 = (f32[8,128]{1,0:T(8,128)S(1)}, f32[8,128]{1,0:T(8,128)S(1)}, u32[]{:S(2)}, u32[]{:S(2)}) collective-permute-start(f32[8,128]{1,0:T(8,128)S(1)} %get-tuple-element.33), channel_id=1, source_target_pairs={{0,1},{1,0},{2,3},{3,2},{4,5},{5,4},{6,7},{7,6},{8,9},{9,8},{10,11... | collective-permute-start | bytes 12296 | tf_op jit(solution)/shard_map/ppermute | solution.py:676
  39.3 5.4 %collective-permute-start.11 = (f32[8,128]{1,0:T(8,128)S(1)}, f32[8,128]{1,0:T(8,128)S(1)}, u32[]{:S(2)}, u32[]{:S(2)}) collective-permute-start(f32[8,128]{1,0:T(8,128)S(1)} %add.16.args_0_), channel_id=1, source_target_pairs={{0,6},{1,7},{2,4},{3,5},{4,2},{5,3},{6,0},{7,1},{8,14},{9,15},{10,... | collective-permute-start | bytes 12296 | tf_op jit(solution)/shard_map/ppermute | solution.py:676
  42.9 4.5 %collective-permute-start.10 = (f32[8,128]{1,0:T(8,128)S(1)}, f32[8,128]{1,0:T(8,128)S(1)}, u32[]{:S(2)}, u32[]{:S(2)}) collective-permute-start(f32[8,128]{1,0:T(8,128)S(1)} %add.16.args_0_), channel_id=1, source_target_pairs={{0,4},{1,5},{2,6},{3,7},{4,0},{5,1},{6,2},{7,3},{8,12},{9,13},{10,... | collective-permute-start | bytes 12296 | tf_op jit(solution)/shard_map/ppermute | solution.py:676
  43.2 4.1 %collective-permute-start.9 = (f32[8,128]{1,0:T(8,128)S(1)}, f32[8,128]{1,0:T(8,128)S(1)}, u32[]{:S(2)}, u32[]{:S(2)}) collective-permute-start(f32[8,128]{1,0:T(8,128)S(1)} %add.16.args_0_), channel_id=1, source_target_pairs={{0,2},{1,3},{2,0},{3,1},{4,6},{5,7},{6,4},{7,5},{8,10},{9,11},{10,... | collective-permute-start | bytes 12296 | tf_op jit(solution)/shard_map/ppermute | solution.py:676
